TPU v7x, 512 devices: a whole 4x8x8 slice. The times are simulated.
512 devices in a mesh: row: 16 (over z, core), head: 32 (over y, x).
Axes of the slice: x: 4, y: 8, z: 8, core: 2. Of those that a mesh axis runs over, the one named last changes fastest.
Arguments:
- hidden: bfloat16 [32, 8192], P(None, 'row'), may hold values from -12 to 12
- norm_gain: bfloat16 [8192], P('row'), may hold values from 0.5 to 1.5
- input_weight: bfloat16 [8192, 2, 16384], P('row', None, 'head'), may hold values from -0.0625 to 0.0625
- group_weight: bfloat16 [8192, 4096], P('row', 'head'), may hold values from -0.0625 to 0.0625
- step_weight: bfloat16 [8192, 256], P('row', 'head'), may hold values from -0.0625 to 0.0625
- conv_inner_weight: bfloat16 [4, 16384], P(None, 'head'), may hold values from -3 to 3
- conv_group_weight: bfloat16 [4, 4096], P(None, 'head'), may hold values from -3 to 3
- conv_inner_state: bfloat16 [32, 3, 16384], P('row', None, 'head'), may hold values from -6 to 6
- conv_group_state: bfloat16 [32, 3, 4096], P('row', None, 'head'), may hold values from -6 to 6
- timestep_bias: float32 [256], P('head'), may hold values from -3 to 0.5
- decay_log: float32 [256], P('head'), may hold values from -1 to 2
- skip_gain: float32 [256], P('head'), may hold values from 0.5 to 1.5
- recurrent_state: bfloat16 [32, 256, 64, 256], P('row', 'head'), may hold values from -6 to 6
- mixer_gain: bfloat16 [16384], P('head'), may hold values from 0.5 to 1.5
- output_weight: bfloat16 [16384, 8192], P('head', 'row'), may hold values from -0.046875 to 0.046875
- final_gain: bfloat16 [8192], P('row'), may hold values from 0.5 to 1.5
- lexicon_matrix: bfloat16 [8192, 65536], P('row', 'head'), may hold values from -0.4375 to 0.4375
- token_mask: int32 [32, 65536], P('row', 'head'), may hold values 0 or 1
- min_share: int32 [32], P('row'), may hold values from 1311 to 13107
Outputs:
- next_state: bfloat16 [32, 256, 64, 256], P('row', 'head')
- next_conv_inner: bfloat16 [32, 3, 16384], P('row', None, 'head')
- next_conv_group: bfloat16 [32, 3, 4096], P('row', None, 'head')
- layer_out: bfloat16 [32, 8192], P(None, 'row')
- next_probs: bfloat16 [32, 65536], P('row', 'head')
Inputs may be any that keep to these rules, and one draw needn't show every extreme that they name: `min_share`: the smallest share of the row's top probability that a token keeps in full at twice that share, times 65536.
All inputs are finite; a program needn't handle non-finite values. No bound on the sum of `token_mask` on one device may be relied on, other than what follows from the above.
Results may differ from a plain program's by a relative error of at most 0.04.
Values may be sent and summed in bfloat16 or wider, within the bound.
A program may use at most 64 MiB of HBM per device.

v0:
```python
import jax
import jax.numpy as jnp
from jax import lax
from jax.sharding import PartitionSpec as P

D = 8192
HEADS = 256
HEAD_DIM = 64
GROUPS = 8


EPSILON = 1e-05
INVERSE_HEAT = 1.25
FIXED_POINT = 65536.0
NEG_LARGE = -1e30


def conv_step(history, newest, filter_coefficient):
    window = jnp.concatenate([history, newest[:, None, :]], axis=1)
    mixed_taps = jnp.sum(
        window.astype(jnp.float32) * filter_coefficient.astype(jnp.float32)[None, :, :], axis=1
    )
    return (window[:, 1:, :], jax.nn.silu(mixed_taps))


def local(
    hidden,
    norm_gain,
    input_weight,
    group_weight,
    step_weight,
    conv_inner_weight,
    conv_group_weight,
    conv_inner_state,
    conv_group_state,
    timestep_bias,
    decay_log,
    skip_gain,
    recurrent_state,
    mixer_gain,
    output_weight,
    final_gain,
    lexicon_matrix,
    token_mask,
    min_share,
):
    rows_mine, heads_mine, head_width, state_width = recurrent_state.shape
    inner_mine = heads_mine * head_width
    head_devices = lax.axis_size("head")
    group_devices = head_devices // GROUPS
    head_index = lax.axis_index("head")
    hidden_wide = hidden.astype(jnp.float32)
    quadratic_accumulated = lax.psum(jnp.sum(hidden_wide * hidden_wide, axis=1), "row")
    hidden_scale = lax.rsqrt(quadratic_accumulated / D + EPSILON)
    normed = (hidden_wide * hidden_scale[:, None] * norm_gain.astype(jnp.float32)[None, :]).astype(
        jnp.bfloat16
    )
    flat_input = input_weight.reshape(input_weight.shape[0], 2 * inner_mine)
    pair_mine = group_weight.shape[1]
    row_block = normed
    projected = lax.psum_scatter(
        jnp.concatenate(
            [
                jnp.dot(row_block, flat_input, preferred_element_type=jnp.float32),
                jnp.dot(row_block, group_weight, preferred_element_type=jnp.float32),
                jnp.dot(row_block, step_weight, preferred_element_type=jnp.float32),
            ],
            axis=1,
        ),
        "row",
        scatter_dimension=0,
        tiled=True,
    )
    gate_raw = projected[:, :inner_mine]
    inner_raw = projected[:, inner_mine : 2 * inner_mine]
    group_raw = projected[:, 2 * inner_mine : 2 * inner_mine + pair_mine]
    step_raw = projected[:, 2 * inner_mine + pair_mine :]
    next_conv_inner, conv_inner = conv_step(
        conv_inner_state, inner_raw.astype(jnp.bfloat16), conv_inner_weight
    )
    next_conv_group, conv_group = conv_step(
        conv_group_state, group_raw.astype(jnp.bfloat16), conv_group_weight
    )
    group_round = conv_group.astype(jnp.bfloat16)
    every_group = lax.all_gather(group_round, "head", axis=1, tiled=True)
    group_index = head_index // group_devices
    group_layout = every_group.reshape(rows_mine, 2 * state_width, GROUPS)
    group_pair = lax.dynamic_slice_in_dim(group_layout, group_index, 1, 2)[:, :, 0]
    pair_wide = group_pair.astype(jnp.float32)
    state_input = pair_wide[:, :state_width]
    state_readout = pair_wide[:, state_width:]
    step_size = jax.nn.softplus(step_raw + timestep_bias[None, :])
    decay_rate = jnp.exp(-step_size * jnp.exp(decay_log)[None, :])
    inner_heads = conv_inner.reshape(rows_mine, heads_mine, head_width)
    state_new = (
        decay_rate[:, :, None, None] * recurrent_state.astype(jnp.float32)
        + (step_size[:, :, None] * inner_heads)[:, :, :, None] * state_input[:, None, None, :]
    )
    readout = jnp.sum(state_new * state_readout[:, None, None, :], axis=3)
    readout = readout + skip_gain[None, :, None] * inner_heads
    gated_out = readout.reshape(rows_mine, inner_mine) * jax.nn.silu(gate_raw)
    local_squares = jnp.sum(gated_out * gated_out, axis=1)
    selector = (jnp.arange(GROUPS) == group_index).astype(jnp.float32)
    group_table = lax.psum(local_squares[:, None] * selector[None, :], "head")
    group_total = jnp.sum(group_table * selector[None, :], axis=1)
    group_scale = lax.rsqrt(group_total / (HEADS * HEAD_DIM // GROUPS) + EPSILON)
    mixer_in = (gated_out * group_scale[:, None] * mixer_gain.astype(jnp.float32)[None, :]).astype(
        jnp.bfloat16
    )
    mixer_part = jnp.dot(
        lax.all_gather(mixer_in, "row", axis=0, tiled=True),
        output_weight,
        preferred_element_type=jnp.float32,
    )
    final_scale = final_gain.astype(jnp.float32)[None, :]
    mixed_complete = lax.psum(mixer_part, "head")
    layer_out = (hidden_wide + mixed_complete).astype(jnp.bfloat16)
    out_wide = layer_out.astype(jnp.float32)
    out_squares = lax.psum(jnp.sum(out_wide * out_wide, axis=1), "row")
    last_rescaled_vector = (
        out_wide * lax.rsqrt(out_squares / D + EPSILON)[:, None] * final_scale
    ).astype(jnp.bfloat16)
    row_block = last_rescaled_vector
    candidate_scores = (
        lax.psum_scatter(
            jnp.dot(row_block, lexicon_matrix, preferred_element_type=jnp.float32),
            "row",
            scatter_dimension=0,
            tiled=True,
        )
        * INVERSE_HEAT
    )
    allowed = token_mask > 0
    peak_logit = lax.pmax(jnp.max(jnp.where(allowed, candidate_scores, NEG_LARGE), axis=1), "head")
    ratio_to_peak = jnp.where(allowed, jnp.exp(candidate_scores - peak_logit[:, None]), 0.0)
    floor_share = min_share.astype(jnp.float32)[:, None] / FIXED_POINT
    weights = ratio_to_peak * jnp.clip(ratio_to_peak / floor_share - 1.0, 0.0, 1.0)
    kept_total = lax.psum(jnp.sum(weights, axis=1), "head")
    next_probs = (weights / kept_total[:, None]).astype(jnp.bfloat16)
    return (state_new.astype(jnp.bfloat16), next_conv_inner, next_conv_group, layer_out, next_probs)


def solution(mesh):
    in_specs = (
        P(None, "row"),
        P("row"),
        P("row", None, "head"),
        P("row", "head"),
        P("row", "head"),
        P(None, "head"),
        P(None, "head"),
        P("row", None, "head"),
        P("row", None, "head"),
        P("head"),
        P("head"),
        P("head"),
        P("row", "head", None, None),
        P("head"),
        P("head", "row"),
        P("row"),
        P("row", "head"),
        P("row", "head"),
        P("row"),
    )
    out_specs = (
        P("row", "head", None, None),
        P("row", None, "head"),
        P("row", None, "head"),
        P(None, "row"),
        P("row", "head"),
    )
    return jax.shard_map(local, mesh=mesh, in_specs=in_specs, out_specs=out_specs, check_vma=False)
```

profile of v0, /device:TPU:2, one launch (start us, length us, event | category | flops | bytes accessed | tf_op | source)
XLA Modules:
  0.0 716.1 jit_solution(9288423445431166698)
XLA Ops:
  7.2 0.0 copy-start
  7.2 0.0 copy-start.3
  7.3 0.0 all-reduce.8.cloned.1.call-start
  7.3 0.8 convert_element_type.70
  8.1 0.9 fusion.4
  9.0 32.0 %psum.35 = f32[32]{0:T(128)S(1)} all-reduce(f32[32]{0:T(128)S(1)} %fusion.4), channel_id=1, replica_groups=mesh['row'=16,'head'=32] {'row'}, use_global_device_ids=true, to_apply=%region_1.0 | all-reduce | flops 32 | bytes 256 | tf_op jit(solution)/shard_map/psum | solution.py:53
  41.0 1.5 copy.30
  42.6 0.3 fusion.21
  42.9 0.2 fusion.17
  43.1 0.2 fusion.19
  43.3 0.7 pad_maximum_fusion
  44.0 0.0 all-reduce.8.cloned.1.call-update
  44.1 0.0 all-reduce.6.cloned.1.call-start
  44.2 0.1 mul.207
  44.3 0.1 mul.208
  44.4 1.3 dynamic-slice
  46.3 102.0 %all-reduce.8.cloned.1.call-done = f32[32,1160]{1,0:T(8,128)} async-done(((f32[32,1160]{1,0:T(8,128)}), f32[32,1160]{1,0:T(8,128)}) %all-reduce.8.cloned.1.call-update) | async-done | bytes 148496
  148.3 0.8 dynamic-slice_convert_fusion
  149.2 34.4 %all_gather.6 = bf16[2,4096]{1,0:T(2,128)(2,1)S(1)} all-gather(bf16[2,128]{1,0:T(2,128)(2,1)S(1)} %fusion.16), channel_id=1, replica_groups=mesh['row'=16,'head'=32] {'head'}, dimensions={1}, use_global_device_ids=true | all-gather | bytes 16896 | tf_op jit(solution)/shard_map/all_gather | solution.py:85
  183.6 0.3 reshape.66
  183.9 0.3 convert_reduce_fusion
  184.2 0.1 reduce_sum.78
  184.3 0.8 multiply_exponential_fusion
  185.1 0.1 multiply_multiply_fusion
  185.1 1.1 multiply_reduce_fusion
  186.3 0.1 reduce_sum.81
  186.3 0.9 multiply_reduce_fusion.2
  187.2 0.1 broadcast_multiply_fusion
  187.3 71.3 %psum.36 = f32[2,8]{1,0:T(2,128)S(1)} all-reduce(f32[2,8]{1,0:T(2,128)S(1)} %broadcast_multiply_fusion), channel_id=1, replica_groups=mesh['row'=16,'head'=32] {'head'}, use_global_device_ids=true, to_apply=%region_7.8 | all-reduce | flops 16 | bytes 128 | tf_op jit(solution)/shard_map/psum | solution.py:104
  258.6 0.1 multiply_reduce_fusion.4
  258.7 0.1 fusion.14
  258.8 15.5 %all-gather = bf16[16,2,512]{2,1,0:T(2,128)(2,1)S(1)} all-gather(bf16[1,2,512]{2,1,0:T(2,128)(2,1)S(1)} %fusion.14), channel_id=1, replica_groups=mesh['row'=16,'head'=32] {'row'}, dimensions={0}, use_global_device_ids=true | all-gather | bytes 34816 | tf_op jit(solution)/shard_map/all_gather | solution.py:111
  274.3 0.8 fusion.27
  275.1 0.0 all-reduce.6.cloned.1.call-update
  275.2 0.0 all-reduce.10.cloned.1.call-start
  275.2 147.2 %all-reduce.6.cloned.1.call-done = f32[32,512]{1,0:T(8,128)} async-done(((f32[32,512]{1,0:T(8,128)}), f32[32,512]{1,0:T(8,128)}) %all-reduce.6.cloned.1.call-update) | async-done | bytes 65552 | tf_op jit(solution)/shard_map/psum | solution.py:116
  422.4 1.0 fusion.1
  423.4 24.2 %psum.38 = f32[32]{0:T(128)S(1)} all-reduce(f32[32]{0:T(128)S(1)} %get-tuple-element.7), channel_id=1, replica_groups=mesh['row'=16,'head'=32] {'row'}, use_global_device_ids=true, to_apply=%region_11.12 | all-reduce | flops 32 | bytes 256 | tf_op jit(solution)/shard_map/psum | solution.py:119
  447.6 1.2 fusion.8
  448.8 0.0 all-reduce.10.cloned.1.call-update
  448.8 0.6 fusion.12
  449.5 112.1 %all-reduce.10.cloned.1.call-done = f32[32,2048]{1,0:T(8,128)} async-done(((f32[32,2048]{1,0:T(8,128)}), f32[32,2048]{1,0:T(8,128)}) %all-reduce.10.cloned.1.call-update) | async-done | bytes 262160
  561.5 1.0 select_reduce_fusion
  562.5 0.6 fusion.15
  563.1 70.6 %pmax.7 = f32[2]{0:T(128)S(1)} all-reduce(f32[2]{0:T(128)S(1)} %select_reduce_fusion), channel_id=1, replica_groups=mesh['row'=16,'head'=32] {'head'}, use_global_device_ids=true, to_apply=%region_14.15 | all-reduce | flops 2 | bytes 16 | tf_op jit(solution)/shard_map/pmax | solution.py:134
  633.7 1.1 fusion.23
  634.8 74.1 %psum.39 = f32[2]{0:T(128)S(1)} all-reduce(f32[2]{0:T(128)S(1)} %get-tuple-element.5), channel_id=1, replica_groups=mesh['row'=16,'head'=32] {'head'}, use_global_device_ids=true, to_apply=%region_16.17 | all-reduce | flops 2 | bytes 16 | tf_op jit(solution)/shard_map/psum | solution.py:138
  708.9 0.7 divide_convert_fusion
  (51 shorter events, 0.2 us)
Async XLA Ops:
  7.2 440.4 %copy-start = (bf16[512,2048]{1,0:T(8,128)(2,1)S(1)}, bf16[512,2048]{1,0:T(8,128)(2,1)}, u32[]{:S(2)}) copy-start(bf16[512,2048]{1,0:T(8,128)(2,1)} %param.35) | copy-start | bytes 6291460
  7.2 35.4 %copy-start.3 = (bf16[32,512]{1,0:T(8,128)(2,1)S(1)}, bf16[32,512]{1,0:T(8,128)(2,1)}, u32[]{:S(2)}) copy-start(bf16[32,512]{1,0:T(8,128)(2,1)} %param.19) | copy-start | bytes 98308
  7.2 35.8 %copy-start.15 = (bf16[512,8]{0,1:T(8,128)(2,1)S(1)}, bf16[512,8]{0,1:T(8,128)(2,1)}, u32[]{:S(2)}) copy-start(bf16[512,8]{0,1:T(8,128)(2,1)} %param.23) | copy-start | bytes 24580
  7.2 35.9 %copy-start.14 = (bf16[512,128]{1,0:T(8,128)(2,1)S(1)}, bf16[512,128]{1,0:T(8,128)(2,1)}, u32[]{:S(2)}) copy-start(bf16[512,128]{1,0:T(8,128)(2,1)} %param.22) | copy-start | bytes 393220
  7.2 36.9 %copy-start.9 = (bf16[4,128]{1,0:T(4,128)(2,1)S(1)}, bf16[4,128]{1,0:T(4,128)(2,1)}, u32[]{:S(2)}) copy-start(bf16[4,128]{1,0:T(4,128)(2,1)} %param.25) | copy-start | bytes 3076
  7.2 36.9 %copy-start.8 = (bf16[4,512]{1,0:T(4,128)(2,1)S(1)}, bf16[4,512]{1,0:T(4,128)(2,1)}, u32[]{:S(2)}) copy-start(bf16[4,512]{1,0:T(4,128)(2,1)} %param.24) | copy-start | bytes 12292
  7.2 36.9 %copy-start.16 = (f32[8]{0:T(128)S(1)}, f32[8]{0:T(128)}, u32[]{:S(2)}) copy-start(f32[8]{0:T(128)} %param.29) | copy-start | bytes 100
  7.2 37.0 %copy-start.12 = (f32[8]{0:T(128)S(1)}, f32[8]{0:T(128)}, u32[]{:S(2)}) copy-start(f32[8]{0:T(128)} %param.30) | copy-start | bytes 100
  7.3 141.1 %all-reduce.8.cloned.1.call-start = ((), (), s32[]{:S(2)}) async-start(), calls=%async_computation.1 | async-start | bytes 327680
  41.0 108.1 %copy-start.7 = (bf16[2,3,128]{2,0,1:T(2,128)(2,1)S(1)}, bf16[2,3,128]{2,0,1:T(2,128)(2,1)}, u32[]{:S(2)}) copy-start(bf16[2,3,128]{2,0,1:T(2,128)(2,1)} %param.27) | copy-start | bytes 4612
  41.0 143.2 %copy-start.6 = (bf16[2,3,512]{2,0,1:T(2,128)(2,1)S(1)}, bf16[2,3,512]{2,0,1:T(2,128)(2,1)}, u32[]{:S(2)}) copy-start(bf16[2,3,512]{2,0,1:T(2,128)(2,1)} %param.26) | copy-start | bytes 18436
  41.0 143.3 %copy-start.13 = (f32[8]{0:T(128)S(1)}, f32[8]{0:T(128)}, u32[]{:S(2)}) copy-start(f32[8]{0:T(128)} %param.28) | copy-start | bytes 100
  41.0 144.1 %copy-start.1 = (bf16[2,8,64,256]{3,2,1,0:T(8,128)(2,1)S(1)}, bf16[2,8,64,256]{3,2,1,0:T(8,128)(2,1)}, u32[]{:S(2)}) copy-start(bf16[2,8,64,256]{3,2,1,0:T(8,128)(2,1)} %param.31) | copy-start | bytes 1572868
  42.6 144.7 %copy-start.10 = (bf16[512]{0:T(512)(128)(2,1)S(1)}, bf16[512]{0:T(512)(128)(2,1)}, u32[]{:S(2)}) copy-start(bf16[512]{0:T(512)(128)(2,1)} %param.32) | copy-start | bytes 3076
  42.6 231.7 %copy-start.2 = (bf16[512,512]{1,0:T(8,128)(2,1)S(1)}, bf16[512,512]{1,0:T(8,128)(2,1)}, u32[]{:S(2)}) copy-start(bf16[512,512]{1,0:T(8,128)(2,1)} %param.33) | copy-start | bytes 1572868
  42.6 232.6 %copy-start.11 = (bf16[512]{0:T(512)(128)(2,1)S(1)}, bf16[512]{0:T(512)(128)(2,1)}, u32[]{:S(2)}) copy-start(bf16[512]{0:T(512)(128)(2,1)} %param.34) | copy-start | bytes 3076
  44.1 378.4 %all-reduce.6.cloned.1.call-start = ((), (), s32[]{:S(2)}) async-start(), calls=%async_computation | async-start | bytes 131072 | tf_op jit(solution)/shard_map/psum | solution.py:116
  185.1 263.7 %copy-start.17 = (s32[2]{0:T(128)S(1)}, s32[2]{0:T(128)}, u32[]{:S(2)}) copy-start(s32[2]{0:T(128)} %param.37) | copy-start | bytes 28
  186.3 375.3 %copy-start.5 = (s32[2,2048]{1,0:T(2,128)S(1)}, s32[2,2048]{1,0:T(2,128)}, u32[]{:S(2)}) copy-start(s32[2,2048]{1,0:T(2,128)} %param.36) | copy-start | bytes 49156
  275.2 286.4 %all-reduce.10.cloned.1.call-start = ((), (), s32[]{:S(2)}) async-start(), calls=%async_computation.2 | async-start | bytes 524288
  423.4 286.2 %copy-start.4 = (bf16[32,512]{1,0:T(8,128)(2,1)}, bf16[32,512]{1,0:T(8,128)(2,1)S(1)}, u32[]{:S(2)}) copy-start(bf16[32,512]{1,0:T(8,128)(2,1)S(1)} %get-tuple-element.8) | copy-start | bytes 98308
Sparse Core Ops, SparseCore 0:
  44.2 104.1 all-reduce.7
  275.3 147.0 all-reduce.5
  448.9 112.5 all-reduce.9
where the time goes:
time: 717 us; the launch traced here: 716 us
  waiting for transfers between devices  361 us (50%)
  blocking collectives  322 us (45%)
  between operations  14.7 us (2%)
  other arithmetic  10.7 us (1%)
    unnamed x5, waiting for transfers between devices  214 us
    psum x1, waiting for transfers between devices, local(): mixed_complete = lax.psum(mixer_part, 'head')  147 us
    psum x1, blocking collectives, local(): kept_total = lax.psum(jnp.sum(weights, axis=1), 'head')  74.1 us
    psum x1, blocking collectives, local(): group_table = lax.psum(local_squares[:, None] * selector[None, :], 'head')  71.3 us
    pmax x1, blocking collectives, local(): lax.pmax(jnp.max(jnp.where(allowed, candidate_scores, NEG_LARGE), axis=1)...  70.6 us
    all_gather x1, blocking collectives, local(): every_group = lax.all_gather(group_round, 'head', axis=1, tiled=True)  34.4 us
    psum x1, blocking collectives, local(): lax.psum(jnp.sum(hidden_wide * hidden_wide, axis=1), 'row')  32 us
    psum x1, blocking collectives, local(): out_squares = lax.psum(jnp.sum(out_wide * out_wide, axis=1), 'row')  24.2 us
  transfers between devices with their start and end apart: 3, of which 3 were waited for; matrix products, arithmetic and copies ran while one was open for 0% of the time, Pallas kernels for 0%

commit v1 on v0

v1 whole, which is shorter than its diff:
```python
import jax
import jax.numpy as jnp
from jax import lax
from jax.experimental import pallas as pl
from jax.experimental.pallas import tpu as pltpu
from jax.sharding import PartitionSpec as P

D = 8192
HEADS = 256
HEAD_DIM = 64
STATE = 256
GROUPS = 8
NR = 16
NH = 32
ROWS = 32
EPSILON = 1e-05
INVERSE_HEAT = 1.25
FIXED_POINT = 65536.0
NEG_LARGE = -1e30
MESH = pl.DeviceIdType.MESH
BF = jnp.bfloat16
F32 = jnp.float32


def silu(v):
    return v / (1.0 + jnp.exp(-v))


def iota(shape, axis):
    return lax.broadcasted_iota(jnp.int32, shape, axis)


def dot(a, b):
    return jnp.dot(a, b, preferred_element_type=F32)


def dot_nt(a, b):
    return lax.dot_general(a, b, (((1,), (1,)), ((), ())), preferred_element_type=F32)


N_IN = 19
SMALL = (
    "hidden",
    "norm_gain",
    "group_weight",
    "step_weight",
    "conv_inner_weight",
    "conv_group_weight",
    "conv_inner_state",
    "conv_group_state",
    "mixer_gain",
    "final_gain",
    "token_mask",
    "recurrent_state",
    "output_weight",
    "lexicon_matrix",
    "timestep_bias",
    "decay_log",
    "skip_gain",
    "min_share",
)


def kernel(
    hidden_h,
    norm_gain_h,
    input_weight_h,
    group_weight_h,
    step_weight_h,
    conv_inner_weight_h,
    conv_group_weight_h,
    conv_inner_state_h,
    conv_group_state_h,
    timestep_bias_h,
    decay_log_h,
    skip_gain_h,
    recurrent_state_h,
    mixer_gain_h,
    output_weight_h,
    final_gain_h,
    lexicon_h,
    token_mask_h,
    min_share_h,
    next_state_h,
    next_conv_inner_h,
    next_conv_group_h,
    layer_out_h,
    next_probs_h,
    hidden_v,
    norm_gain_v,
    input_weight_v,
    group_weight_v,
    step_weight_v,
    conv_inner_weight_v,
    conv_group_weight_v,
    conv_inner_state_v,
    conv_group_state_v,
    recurrent_state_v,
    mixer_gain_v,
    output_weight_v,
    final_gain_v,
    lexicon_v,
    token_mask_v,
    next_state_v,
    next_conv_inner,
    next_conv_group,
    layer_out,
    next_probs,
    timestep_bias,
    decay_log,
    skip_gain,
    min_share,
    hidden_rows,
    square_buf,
    in_part,
    in_buf,
    pair_buf,
    share_buf,
    mixer_buf,
    mixed_part,
    mixed_buf,
    scale_buf,
    out_buf,
    logit_part,
    logit_buf,
    peak_buf,
    total_buf,
    in_sem,
    weight_sem,
    save_sem,
    send_sem,
    recv_sem,
):
    i = lax.axis_index("row")
    j = lax.axis_index("head")

    loads = {
        "hidden": (hidden_h, hidden_v),
        "norm_gain": (norm_gain_h, norm_gain_v),
        "group_weight": (group_weight_h, group_weight_v),
        "step_weight": (step_weight_h, step_weight_v),
        "conv_inner_weight": (conv_inner_weight_h, conv_inner_weight_v),
        "conv_group_weight": (conv_group_weight_h, conv_group_weight_v),
        "conv_inner_state": (conv_inner_state_h, conv_inner_state_v),
        "conv_group_state": (conv_group_state_h, conv_group_state_v),
        "mixer_gain": (mixer_gain_h, mixer_gain_v),
        "final_gain": (final_gain_h, final_gain_v),
        "token_mask": (token_mask_h, token_mask_v),
        "recurrent_state": (recurrent_state_h, recurrent_state_v),
        "output_weight": (output_weight_h, output_weight_v),
        "lexicon_matrix": (lexicon_h, lexicon_v),
        "timestep_bias": (timestep_bias_h, timestep_bias),
        "decay_log": (decay_log_h, decay_log),
        "skip_gain": (skip_gain_h, skip_gain),
        "min_share": (min_share_h, min_share),
    }

    def load(name):
        src, dst = loads[name]
        return pltpu.make_async_copy(src, dst, in_sem.at[SMALL.index(name)])

    def load_weight(block):
        return pltpu.make_async_copy(
            input_weight_h.at[:, :, pl.ds(block * 128, 128)],
            input_weight_v.at[block],
            weight_sem.at[block],
        )

    load("hidden").start()
    load("norm_gain").start()
    for block in range(4):
        load_weight(block).start()
    for name in SMALL[2:]:
        load(name).start()

    barrier = pltpu.get_barrier_semaphore()

    def greet_row(k, carry):
        pl.semaphore_signal(barrier, inc=1, device_id=(lax.rem(i + k, NR), j), device_id_type=MESH)
        return carry

    def greet_head(k, carry):
        pl.semaphore_signal(barrier, inc=1, device_id=(i, lax.rem(j + k, NH)), device_id_type=MESH)
        return carry

    lax.fori_loop(1, NR, greet_row, 0)
    lax.fori_loop(1, NH, greet_head, 0)

    def send_row(phase, src, dst):
        def step(k, carry):
            to = lax.rem(i + k, NR)
            pltpu.make_async_remote_copy(
                src_ref=dst.at[i] if src is None else src.at[to],
                dst_ref=dst.at[i],
                send_sem=send_sem.at[phase],
                recv_sem=recv_sem.at[phase],
                device_id=(to, j),
                device_id_type=MESH,
            ).start()
            return carry

        lax.fori_loop(1, NR, step, 0)

    def send_head(phase, src, dst):
        def step(k, carry):
            to = lax.rem(j + k, NH)
            pltpu.make_async_remote_copy(
                src_ref=dst.at[j] if src is None else src.at[to],
                dst_ref=dst.at[j],
                send_sem=send_sem.at[phase],
                recv_sem=recv_sem.at[phase],
                device_id=(i, to),
                device_id_type=MESH,
            ).start()
            return carry

        lax.fori_loop(1, NH, step, 0)

    def arrived(phase, dst):
        rest = dst.at[pl.ds(0, dst.shape[0] - 1)]
        pltpu.make_async_copy(rest, rest, recv_sem.at[phase]).wait()

    def sent(phase, dst):
        rest = dst.at[pl.ds(0, dst.shape[0] - 1)]
        pltpu.make_async_copy(rest, rest, send_sem.at[phase]).wait()

    def send_group(phase, dst):
        first = j - j % 4

        def step(k, carry):
            to = first + lax.rem(j + k, 4)
            pltpu.make_async_remote_copy(
                src_ref=dst.at[j % 4],
                dst_ref=dst.at[j % 4],
                send_sem=send_sem.at[phase],
                recv_sem=recv_sem.at[phase],
                device_id=(i, to),
                device_id_type=MESH,
            ).start()
            return carry

        lax.fori_loop(1, 4, step, 0)

    def save(at, src, dst):
        copy = pltpu.make_async_copy(src, dst, save_sem.at[at])
        copy.start()
        return copy

    load("hidden").wait()
    load("norm_gain").wait()
    hidden_wide = hidden_v[...].astype(F32)
    hidden_rows[:, 0, :] = hidden_wide
    squares = jnp.sum(hidden_wide * hidden_wide, axis=1, keepdims=True)
    diagonal = iota((ROWS, 128), 0) == iota((ROWS, 128), 1)
    square_buf[i] = jnp.sum(jnp.where(diagonal, squares, 0.0), axis=0, keepdims=True)
    pl.semaphore_wait(barrier, NR + NH - 2)
    send_row(8, None, square_buf)
    arrived(8, square_buf)
    square_total = jnp.sum(square_buf[:, 0, :], axis=0, keepdims=True)
    row_total = jnp.sum(jnp.where(diagonal, square_total, 0.0), axis=1, keepdims=True)
    hidden_scale = lax.rsqrt(row_total / D + EPSILON)

    gained = (hidden_wide * hidden_scale * norm_gain_v[...].astype(F32).reshape(1, 512)).astype(BF)
    depth_at, slot_at = iota((128, 256), 0), iota((128, 256), 1)
    spread_even = (slot_at == 2 * depth_at).astype(F32).astype(BF)
    spread_odd = (slot_at == 2 * depth_at + 1).astype(F32).astype(BF)
    blocks = [gained[:, 128 * b : 128 * b + 128] for b in range(4)]
    doubled = jnp.concatenate(
        [
            jnp.concatenate([dot(part, spread_even) for part in blocks], axis=1),
            jnp.concatenate([dot(part, spread_odd) for part in blocks], axis=1),
        ],
        axis=0,
    ).astype(BF)
    for block in range(4):
        load_weight(block).wait()
        both = dot(doubled, input_weight_v[block].reshape(1024, 128))
        in_part[:, :, 128 * block : 128 * block + 128] = both[:32].reshape(NR, 2, 128)
        in_part[:, :, 512 + 128 * block : 640 + 128 * block] = both[32:].reshape(NR, 2, 128)
    load("group_weight").wait()
    in_part[:, :, 1024:1152] = dot(gained, group_weight_v[...]).reshape(NR, 2, 128)
    load("step_weight").wait()
    step_rows = jnp.concatenate(
        [step_weight_v[...].astype(F32), jnp.zeros((120, 512), F32)], axis=0
    ).astype(BF)
    in_part[:, :, 1152:1280] = dot_nt(gained, step_rows).reshape(NR, 2, 128)
    send_row(0, in_part, in_buf)
    in_buf[i] = in_part[i]

    for name in ("conv_inner_weight", "conv_group_weight", "conv_inner_state", "conv_group_state"):
        load(name).wait()
    arrived(0, in_buf)
    projected = jnp.sum(in_buf[...], axis=0)
    group_new = (projected[:, 1024:1152]).astype(BF)
    group_old = conv_group_state_v[...].astype(F32)
    group_taps = conv_group_weight_v[...].astype(F32)
    group_mix = (
        group_old[0] * group_taps[0:1]
        + group_old[1] * group_taps[1:2]
        + group_old[2] * group_taps[2:3]
        + group_new.astype(F32) * group_taps[3:4]
    )
    pair_buf[j] = silu(group_mix).astype(BF).astype(F32)
    send_head(1, None, pair_buf)

    next_conv_group[0] = conv_group_state_v[1]
    next_conv_group[1] = conv_group_state_v[2]
    next_conv_group[2] = group_new
    inner_new = (projected[:, 512:1024]).astype(BF)
    next_conv_inner[0] = conv_inner_state_v[1]
    next_conv_inner[1] = conv_inner_state_v[2]
    next_conv_inner[2] = inner_new
    inner_old = conv_inner_state_v[...].astype(F32)
    inner_taps = conv_inner_weight_v[...].astype(F32)
    conv_inner = silu(
        inner_old[0] * inner_taps[0:1]
        + inner_old[1] * inner_taps[1:2]
        + inner_old[2] * inner_taps[2:3]
        + inner_new.astype(F32) * inner_taps[3:4]
    )
    gate = silu(projected[:, :512])
    step_raw = projected[:, 1152:1160]
    saves = [
        save(1, next_conv_inner, next_conv_inner_h),
        save(2, next_conv_group, next_conv_group_h),
    ]
    for name in ("timestep_bias", "decay_log", "skip_gain"):
        load(name).wait()
    head_of = iota((2, 512), 1) // HEAD_DIM
    step_in = jnp.zeros((2, 512), F32)
    rate_log = jnp.zeros((2, 512), F32)
    skip = jnp.zeros((2, 512), F32)
    for h in range(8):
        here = head_of == h
        step_in = jnp.where(here, step_raw[:, h : h + 1] + timestep_bias[h], step_in)
        rate_log = jnp.where(here, decay_log[h], rate_log)
        skip = jnp.where(here, skip_gain[h], skip)
    step_size = jnp.maximum(step_in, 0.0) + jnp.log1p(jnp.exp(-jnp.abs(step_in)))
    decay = jnp.exp(-step_size * jnp.exp(rate_log))
    driven = step_size * conv_inner

    group_at = j // (NH // GROUPS)
    channel_at, entry_at = iota((128, 256), 0), iota((128, 256), 1)
    pick = (channel_at == (entry_at % 16) * GROUPS + group_at).astype(F32).astype(BF)
    source_at, entry_of = iota((NH, 256), 0), iota((NH, 256), 1) // 16
    load("recurrent_state").wait()
    load("mixer_gain").wait()
    arrived(1, pair_buf)
    inputs, readouts = [], []
    for r in range(2):
        picked = dot(pair_buf[:, r, :].astype(BF), pick)
        inputs.append(
            jnp.sum(jnp.where(source_at == entry_of, picked, 0.0), axis=0, keepdims=True)
        )
        readouts.append(
            jnp.sum(jnp.where(source_at == entry_of + 16, picked, 0.0), axis=0, keepdims=True)
        )
    readout = []
    for r in range(2):
        old_read = dot_nt(readouts[r].astype(BF), recurrent_state_v[r].reshape(512, 256))
        pair_dot = jnp.sum(inputs[r] * readouts[r], axis=1, keepdims=True)
        readout.append(
            decay[r : r + 1] * old_read
            + driven[r : r + 1] * pair_dot
            + skip[r : r + 1] * conv_inner[r : r + 1]
        )
    gated = jnp.concatenate(readout, axis=0) * gate
    gated_squares = jnp.sum(gated * gated, axis=1, keepdims=True)
    mixer_gain_wide = mixer_gain_v[...].astype(F32).reshape(1, 512)
    share_buf[j % 4] = jnp.broadcast_to(gated_squares, (2, 128))
    send_group(9, share_buf)
    arrived(9, share_buf)
    group_total = jnp.sum(share_buf[...], axis=0)[:, 0:1]
    group_scale = lax.rsqrt(group_total / (HEADS * HEAD_DIM // GROUPS) + EPSILON)
    mixer_buf[i] = (gated * group_scale * mixer_gain_wide).astype(BF).astype(F32)
    send_row(2, None, mixer_buf)

    rows8 = jnp.concatenate([driven, decay, jnp.zeros((4, 512), F32)], axis=0)
    columns = rows8.T
    for r in range(2):
        for h in range(8):
            at = slice(64 * h, 64 * h + 64)
            fresh = (
                columns[at, 2 + r : 3 + r] * recurrent_state_v[r, h].astype(F32)
                + columns[at, r : r + 1] * inputs[r]
            )
            next_state_v[r, h] = fresh.astype(BF)
    saves.append(save(0, next_state_v, next_state_h))

    load("output_weight").wait()
    arrived(2, mixer_buf)
    mixer_rows = mixer_buf[...].reshape(ROWS, 512).astype(BF)
    mixed_part[:, 0, :] = dot(mixer_rows, output_weight_v[...])
    send_head(3, mixed_part, mixed_buf)
    mixed_buf[j] = mixed_part[j]

    arrived(3, mixed_buf)
    mixed = jnp.sum(mixed_buf[:, 0, :], axis=0, keepdims=True)
    out_mine = (hidden_rows[j] + mixed).astype(BF).astype(F32)
    scale_buf[i] = jnp.broadcast_to(jnp.sum(out_mine * out_mine, axis=1, keepdims=True), (1, 128))
    send_row(10, None, scale_buf)
    arrived(10, scale_buf)
    out_buf[j, :, 0:512] = out_mine
    out_buf[j, :, 512:640] = jnp.sum(scale_buf[:, 0, :], axis=0, keepdims=True)
    send_head(4, None, out_buf)

    load("final_gain").wait()
    load("lexicon_matrix").wait()
    load("token_mask").wait()
    load("min_share").wait()
    final_gain_wide = final_gain_v[...].astype(F32).reshape(1, 512)
    arrived(4, out_buf)
    out_wide = out_buf[:, 0, 0:512]
    out_scale = lax.rsqrt(out_buf[:, 0, 512:640][:, 0:1] / D + EPSILON)
    final_rows = (out_wide * out_scale * final_gain_wide).astype(BF)
    for block in range(4):
        at = slice(512 * block, 512 * block + 512)
        logit_part[:, :, at] = dot(final_rows, lexicon_v[:, at]).reshape(NR, 2, 512)
    send_row(5, logit_part, logit_buf)
    logit_buf[i] = logit_part[i]
    layer_out[...] = out_wide.astype(BF)
    saves.append(save(3, layer_out, layer_out_h))

    allowed = token_mask_v[...] > 0
    row_at = iota((2, 1), 0)
    floor_share = (
        jnp.where(row_at == 0, min_share[0], min_share[1]).astype(F32) / FIXED_POINT
    )
    arrived(5, logit_buf)
    scores = jnp.sum(logit_buf[...], axis=0) * INVERSE_HEAT
    peak_mine = jnp.max(jnp.where(allowed, scores, NEG_LARGE), axis=1, keepdims=True)
    peak_buf[j] = jnp.broadcast_to(peak_mine, (2, 128))
    send_head(6, None, peak_buf)
    arrived(6, peak_buf)
    peak = jnp.max(peak_buf[...], axis=0)[:, 0:1]
    ratio = jnp.where(allowed, jnp.exp(scores - peak), 0.0)
    weights = ratio * jnp.clip(ratio / floor_share - 1.0, 0.0, 1.0)
    total_mine = jnp.sum(weights, axis=1, keepdims=True)
    total_buf[j] = jnp.broadcast_to(total_mine, (2, 128))
    send_head(7, None, total_buf)
    arrived(7, total_buf)
    total = jnp.sum(total_buf[...], axis=0)[:, 0:1]
    next_probs[...] = (weights / total).astype(BF)

    saves.append(save(4, next_probs, next_probs_h))
    for copy in saves:
        copy.wait()
    for phase, dst in enumerate(
        (
            in_buf,
            pair_buf,
            mixer_buf,
            mixed_buf,
            out_buf,
            logit_buf,
            peak_buf,
            total_buf,
            square_buf,
            share_buf,
            scale_buf,
        )
    ):
        sent(phase, dst)


def local(
    hidden,
    norm_gain,
    input_weight,
    group_weight,
    step_weight,
    conv_inner_weight,
    conv_group_weight,
    conv_inner_state,
    conv_group_state,
    timestep_bias,
    decay_log,
    skip_gain,
    recurrent_state,
    mixer_gain,
    output_weight,
    final_gain,
    lexicon_matrix,
    token_mask,
    min_share,
):
    hbm = pl.BlockSpec(memory_space=pltpu.HBM)
    in_specs = [hbm] * N_IN
    state, inner, group, out, probs = pl.pallas_call(
        kernel,
        out_shape=(
            jax.ShapeDtypeStruct((2, 8, 64, 256), BF),
            jax.ShapeDtypeStruct((3, 2, 512), BF),
            jax.ShapeDtypeStruct((3, 2, 128), BF),
            jax.ShapeDtypeStruct((ROWS, 512), BF),
            jax.ShapeDtypeStruct((2, 2048), BF),
        ),
        in_specs=in_specs,
        out_specs=(hbm,) * 5,
        scratch_shapes=[
            pltpu.VMEM((ROWS, 512), BF),
            pltpu.VMEM((512,), BF),
            pltpu.VMEM((4, 512, 2, 128), BF),
            pltpu.VMEM((512, 128), BF),
            pltpu.VMEM((8, 512), BF),
            pltpu.VMEM((4, 512), BF),
            pltpu.VMEM((4, 128), BF),
            pltpu.VMEM((3, 2, 512), BF),
            pltpu.VMEM((3, 2, 128), BF),
            pltpu.VMEM((2, 8, 64, 256), BF),
            pltpu.VMEM((512,), BF),
            pltpu.VMEM((512, 512), BF),
            pltpu.VMEM((512,), BF),
            pltpu.VMEM((512, 2048), BF),
            pltpu.VMEM((2, 2048), jnp.int32),
            pltpu.VMEM((2, 8, 64, 256), BF),
            pltpu.VMEM((3, 2, 512), BF),
            pltpu.VMEM((3, 2, 128), BF),
            pltpu.VMEM((ROWS, 512), BF),
            pltpu.VMEM((2, 2048), BF),
            pltpu.SMEM((8,), F32),
            pltpu.SMEM((8,), F32),
            pltpu.SMEM((8,), F32),
            pltpu.SMEM((2,), jnp.int32),
            pltpu.VMEM((ROWS, 1, 512), F32),
            pltpu.VMEM((NR, 1, 128), F32),
            pltpu.VMEM((NR, 2, 1280), F32),
            pltpu.VMEM((NR, 2, 1280), F32),
            pltpu.VMEM((NH, 2, 128), F32),
            pltpu.VMEM((4, 2, 128), F32),
            pltpu.VMEM((NR, 2, 512), F32),
            pltpu.VMEM((ROWS, 1, 512), F32),
            pltpu.VMEM((NH, 1, 512), F32),
            pltpu.VMEM((NR, 1, 128), F32),
            pltpu.VMEM((NH, 1, 640), F32),
            pltpu.VMEM((NR, 2, 2048), F32),
            pltpu.VMEM((NR, 2, 2048), F32),
            pltpu.VMEM((NH, 2, 128), F32),
            pltpu.VMEM((NH, 2, 128), F32),
            pltpu.SemaphoreType.DMA((len(SMALL),)),
            pltpu.SemaphoreType.DMA((4,)),
            pltpu.SemaphoreType.DMA((5,)),
            pltpu.SemaphoreType.DMA((11,)),
            pltpu.SemaphoreType.DMA((11,)),
        ],
        compiler_params=pltpu.CompilerParams(
            collective_id=0, has_side_effects=True, vmem_limit_bytes=56 << 20
        ),
    )(
        hidden,
        norm_gain,
        input_weight,
        group_weight,
        step_weight.T,
        conv_inner_weight,
        conv_group_weight,
        jnp.transpose(conv_inner_state, (1, 0, 2)),
        jnp.transpose(conv_group_state, (1, 0, 2)),
        timestep_bias,
        decay_log,
        skip_gain,
        recurrent_state,
        mixer_gain,
        output_weight,
        final_gain,
        lexicon_matrix,
        token_mask,
        min_share,
    )
    return (
        state,
        jnp.transpose(inner, (1, 0, 2)),
        jnp.transpose(group, (1, 0, 2)),
        out,
        probs,
    )


def solution(mesh):
    in_specs = (
        P(None, "row"),
        P("row"),
        P("row", None, "head"),
        P("row", "head"),
        P("row", "head"),
        P(None, "head"),
        P(None, "head"),
        P("row", None, "head"),
        P("row", None, "head"),
        P("head"),
        P("head"),
        P("head"),
        P("row", "head", None, None),
        P("head"),
        P("head", "row"),
        P("row"),
        P("row", "head"),
        P("row", "head"),
        P("row"),
    )
    out_specs = (
        P("row", "head", None, None),
        P("row", None, "head"),
        P("row", None, "head"),
        P(None, "row"),
        P("row", "head"),
    )
    return jax.shard_map(local, mesh=mesh, in_specs=in_specs, out_specs=out_specs, check_vma=False)
```

time: 717 us -> 88.9 us (0.12)
  the two profiles are of different devices: /device:TPU:2 before, /device:TPU:1 now
where the time goes in v1:
time: 88.9 us; the launch traced here: 88.6 us
  Pallas kernels  80.8 us (91%)
  local copies, waits for them, and re-layouts  7.07 us (8%)
    pallas_call x1, Pallas kernels, local(): pl.pallas_call(kernel, out_shape=(jax.ShapeDtypeStruct((2, 8, 64, 256), B...  80.8 us
    unnamed x5, local copies, waits for them, and re-layouts  7.07 us

profile of v1, /device:TPU:1, one launch (start us, length us, event | category | flops | bytes accessed | tf_op | source)
XLA Modules:
  0.0 88.6 jit_solution(999139520699029939)
XLA Ops:
  0.6 80.8 %shard_map.218 = (bf16[2,8,64,256]{3,2,1,0:T(8,128)(2,1)}, bf16[3,2,512]{2,1,0:T(2,128)(2,1)}, bf16[3,2,128]{2,1,0:T(2,128)(2,1)}, bf16[32,512]{1,0:T(8,128)(2,1)}, bf16[2,2048]{1,0:T(2,128)(2,1)}) custom-call(bf16[32,512]{1,0:T(8,128)(2,1)} %hidden_h.1, bf16[512]{0:T(512)(128)(2,1)} %norm_gain_h.1, bf16[512,2,512]{2,1,0:T(2,128)(2,1)} %input_weight_h.1, ...), custom_call_target="tpu_custom_call" | custom-call | tf_op jit(solution)/shard_map/pallas_call | solution.py:489
  81.5 1.9 %copy.29 = bf16[2,8,64,256]{3,2,1,0:T(8,128)(2,1)} copy(bf16[2,8,64,256]{3,2,1,0:T(8,128)(2,1)} %get-tuple-element.20) | data formatting | bytes 1048576
  83.4 1.3 %copy.30 = bf16[2,3,512]{2,0,1:T(2,128)(2,1)} copy(bf16[2,3,512]{2,0,1:T(2,128)(2,1)} %bitcast.7) | data formatting | bytes 12288
  84.7 1.2 %copy.31 = bf16[2,3,128]{2,0,1:T(2,128)(2,1)} copy(bf16[2,3,128]{2,0,1:T(2,128)(2,1)} %bitcast.9) | data formatting | bytes 3072
  85.9 1.4 %copy.32 = bf16[32,512]{1,0:T(8,128)(2,1)} copy(bf16[32,512]{1,0:T(8,128)(2,1)} %get-tuple-element.23) | data formatting | bytes 65536
  87.3 1.3 %copy.33 = bf16[2,2048]{1,0:T(2,128)(2,1)} copy(bf16[2,2048]{1,0:T(2,128)(2,1)} %get-tuple-element.24) | data formatting | bytes 16384

commit v2 on v1

--- a/solution.py
+++ b/solution.py
@@ -112,6 +112,8 @@
     min_share,
     hidden_rows,
     square_buf,
+    group_part,
+    group_buf,
     in_part,
     in_buf,
     pair_buf,
@@ -175,20 +177,25 @@
 
     barrier = pltpu.get_barrier_semaphore()
 
+    def far_first(k, n):
+        return n // 2 + (2 * (k % 2) - 1) * ((k + 1) // 2)
+
     def greet_row(k, carry):
-        pl.semaphore_signal(barrier, inc=1, device_id=(lax.rem(i + k, NR), j), device_id_type=MESH)
+        to = lax.rem(i + far_first(k, NR), NR)
+        pl.semaphore_signal(barrier, inc=1, device_id=(to, j), device_id_type=MESH)
         return carry
 
     def greet_head(k, carry):
-        pl.semaphore_signal(barrier, inc=1, device_id=(i, lax.rem(j + k, NH)), device_id_type=MESH)
+        to = lax.rem(j + far_first(k, NH), NH)
+        pl.semaphore_signal(barrier, inc=1, device_id=(i, to), device_id_type=MESH)
         return carry
 
-    lax.fori_loop(1, NR, greet_row, 0)
-    lax.fori_loop(1, NH, greet_head, 0)
+    lax.fori_loop(0, NR - 1, greet_row, 0)
+    lax.fori_loop(0, NH - 1, greet_head, 0)
 
     def send_row(phase, src, dst):
         def step(k, carry):
-            to = lax.rem(i + k, NR)
+            to = lax.rem(i + far_first(k, NR), NR)
             pltpu.make_async_remote_copy(
                 src_ref=dst.at[i] if src is None else src.at[to],
                 dst_ref=dst.at[i],
@@ -199,11 +206,11 @@
             ).start()
             return carry
 
-        lax.fori_loop(1, NR, step, 0)
+        lax.fori_loop(0, NR - 1, step, 0)
 
     def send_head(phase, src, dst):
         def step(k, carry):
-            to = lax.rem(j + k, NH)
+            to = lax.rem(j + far_first(k, NH), NH)
             pltpu.make_async_remote_copy(
                 src_ref=dst.at[j] if src is None else src.at[to],
                 dst_ref=dst.at[j],
@@ -214,7 +221,7 @@
             ).start()
             return carry
 
-        lax.fori_loop(1, NH, step, 0)
+        lax.fori_loop(0, NH - 1, step, 0)
 
     def arrived(phase, dst):
         rest = dst.at[pl.ds(0, dst.shape[0] - 1)]
@@ -253,6 +260,10 @@
     squares = jnp.sum(hidden_wide * hidden_wide, axis=1, keepdims=True)
     diagonal = iota((ROWS, 128), 0) == iota((ROWS, 128), 1)
     square_buf[i] = jnp.sum(jnp.where(diagonal, squares, 0.0), axis=0, keepdims=True)
+    depth_at, slot_at = iota((128, 256), 0), iota((128, 256), 1)
+    spread_even = (slot_at == 2 * depth_at).astype(F32).astype(BF)
+    spread_odd = (slot_at == 2 * depth_at + 1).astype(F32).astype(BF)
+    load("group_weight").wait()
     pl.semaphore_wait(barrier, NR + NH - 2)
     send_row(8, None, square_buf)
     arrived(8, square_buf)
@@ -261,9 +272,9 @@
     hidden_scale = lax.rsqrt(row_total / D + EPSILON)
 
     gained = (hidden_wide * hidden_scale * norm_gain_v[...].astype(F32).reshape(1, 512)).astype(BF)
-    depth_at, slot_at = iota((128, 256), 0), iota((128, 256), 1)
-    spread_even = (slot_at == 2 * depth_at).astype(F32).astype(BF)
-    spread_odd = (slot_at == 2 * depth_at + 1).astype(F32).astype(BF)
+    group_part[...] = dot(gained, group_weight_v[...]).reshape(NR, 2, 128)
+    send_row(0, group_part, group_buf)
+    group_buf[i] = group_part[i]
     blocks = [gained[:, 128 * b : 128 * b + 128] for b in range(4)]
     doubled = jnp.concatenate(
         [
@@ -277,21 +288,18 @@
         both = dot(doubled, input_weight_v[block].reshape(1024, 128))
         in_part[:, :, 128 * block : 128 * block + 128] = both[:32].reshape(NR, 2, 128)
         in_part[:, :, 512 + 128 * block : 640 + 128 * block] = both[32:].reshape(NR, 2, 128)
-    load("group_weight").wait()
-    in_part[:, :, 1024:1152] = dot(gained, group_weight_v[...]).reshape(NR, 2, 128)
     load("step_weight").wait()
     step_rows = jnp.concatenate(
         [step_weight_v[...].astype(F32), jnp.zeros((120, 512), F32)], axis=0
     ).astype(BF)
-    in_part[:, :, 1152:1280] = dot_nt(gained, step_rows).reshape(NR, 2, 128)
-    send_row(0, in_part, in_buf)
+    in_part[:, :, 1024:1152] = dot_nt(gained, step_rows).reshape(NR, 2, 128)
+    send_row(11, in_part, in_buf)
     in_buf[i] = in_part[i]
 
     for name in ("conv_inner_weight", "conv_group_weight", "conv_inner_state", "conv_group_state"):
         load(name).wait()
-    arrived(0, in_buf)
-    projected = jnp.sum(in_buf[...], axis=0)
-    group_new = (projected[:, 1024:1152]).astype(BF)
+    arrived(0, group_buf)
+    group_new = jnp.sum(group_buf[...], axis=0).astype(BF)
     group_old = conv_group_state_v[...].astype(F32)
     group_taps = conv_group_weight_v[...].astype(F32)
     group_mix = (
@@ -300,13 +308,15 @@
         + group_old[2] * group_taps[2:3]
         + group_new.astype(F32) * group_taps[3:4]
     )
-    pair_buf[j] = silu(group_mix).astype(BF).astype(F32)
+    pair_buf[j] = silu(group_mix).astype(BF)
     send_head(1, None, pair_buf)
 
     next_conv_group[0] = conv_group_state_v[1]
     next_conv_group[1] = conv_group_state_v[2]
     next_conv_group[2] = group_new
-    inner_new = (projected[:, 512:1024]).astype(BF)
+    arrived(11, in_buf)
+    projected = jnp.sum(in_buf[...], axis=0)
+    inner_new = projected[:, 512:1024].astype(BF)
     next_conv_inner[0] = conv_inner_state_v[1]
     next_conv_inner[1] = conv_inner_state_v[2]
     next_conv_inner[2] = inner_new
@@ -319,7 +329,7 @@
         + inner_new.astype(F32) * inner_taps[3:4]
     )
     gate = silu(projected[:, :512])
-    step_raw = projected[:, 1152:1160]
+    step_raw = projected[:, 1024:1032]
     saves = [
         save(1, next_conv_inner, next_conv_inner_h),
         save(2, next_conv_group, next_conv_group_h),
@@ -348,7 +358,7 @@
     arrived(1, pair_buf)
     inputs, readouts = [], []
     for r in range(2):
-        picked = dot(pair_buf[:, r, :].astype(BF), pick)
+        picked = dot(pair_buf[:, r, :], pick)
         inputs.append(
             jnp.sum(jnp.where(source_at == entry_of, picked, 0.0), axis=0, keepdims=True)
         )
@@ -372,7 +382,7 @@
     arrived(9, share_buf)
     group_total = jnp.sum(share_buf[...], axis=0)[:, 0:1]
     group_scale = lax.rsqrt(group_total / (HEADS * HEAD_DIM // GROUPS) + EPSILON)
-    mixer_buf[i] = (gated * group_scale * mixer_gain_wide).astype(BF).astype(F32)
+    mixer_buf[i] = (gated * group_scale * mixer_gain_wide).astype(BF)
     send_row(2, None, mixer_buf)
 
     rows8 = jnp.concatenate([driven, decay, jnp.zeros((4, 512), F32)], axis=0)
@@ -389,36 +399,37 @@
 
     load("output_weight").wait()
     arrived(2, mixer_buf)
-    mixer_rows = mixer_buf[...].reshape(ROWS, 512).astype(BF)
+    mixer_rows = mixer_buf[...].reshape(ROWS, 512)
     mixed_part[:, 0, :] = dot(mixer_rows, output_weight_v[...])
     send_head(3, mixed_part, mixed_buf)
     mixed_buf[j] = mixed_part[j]
 
+    load("final_gain").wait()
+    final_gain_wide = final_gain_v[...].astype(F32).reshape(1, 512)
     arrived(3, mixed_buf)
     mixed = jnp.sum(mixed_buf[:, 0, :], axis=0, keepdims=True)
-    out_mine = (hidden_rows[j] + mixed).astype(BF).astype(F32)
+    out_rounded = (hidden_rows[j] + mixed).astype(BF)
+    out_mine = out_rounded.astype(F32)
     scale_buf[i] = jnp.broadcast_to(jnp.sum(out_mine * out_mine, axis=1, keepdims=True), (1, 128))
     send_row(10, None, scale_buf)
     arrived(10, scale_buf)
-    out_buf[j, :, 0:512] = out_mine
-    out_buf[j, :, 512:640] = jnp.sum(scale_buf[:, 0, :], axis=0, keepdims=True)
+    out_total = jnp.sum(scale_buf[:, 0, :], axis=0, keepdims=True)[:, 0:1]
+    out_scale = lax.rsqrt(out_total / D + EPSILON)
+    final_mine = (out_mine * out_scale * final_gain_wide).astype(BF).astype(F32)
+    out_buf[j] = jnp.concatenate([final_mine, out_mine], axis=0).astype(BF)
     send_head(4, None, out_buf)
 
-    load("final_gain").wait()
     load("lexicon_matrix").wait()
     load("token_mask").wait()
     load("min_share").wait()
-    final_gain_wide = final_gain_v[...].astype(F32).reshape(1, 512)
     arrived(4, out_buf)
-    out_wide = out_buf[:, 0, 0:512]
-    out_scale = lax.rsqrt(out_buf[:, 0, 512:640][:, 0:1] / D + EPSILON)
-    final_rows = (out_wide * out_scale * final_gain_wide).astype(BF)
+    final_rows = out_buf[:, 0, :]
     for block in range(4):
         at = slice(512 * block, 512 * block + 512)
-        logit_part[:, :, at] = dot(final_rows, lexicon_v[:, at]).reshape(NR, 2, 512)
-    send_row(5, logit_part, logit_buf)
-    logit_buf[i] = logit_part[i]
-    layer_out[...] = out_wide.astype(BF)
+        logit_part[block] = dot(final_rows, lexicon_v[:, at]).reshape(NR, 2, 512)
+        send_row(12 + block, logit_part.at[block], logit_buf.at[block])
+        logit_buf[block, i] = logit_part[block, i]
+    layer_out[...] = out_buf[:, 1, :]
     saves.append(save(3, layer_out, layer_out_h))
 
     allowed = token_mask_v[...] > 0
@@ -426,8 +437,11 @@
     floor_share = (
         jnp.where(row_at == 0, min_share[0], min_share[1]).astype(F32) / FIXED_POINT
     )
-    arrived(5, logit_buf)
-    scores = jnp.sum(logit_buf[...], axis=0) * INVERSE_HEAT
+    sums = []
+    for block in range(4):
+        arrived(12 + block, logit_buf.at[block])
+        sums.append(jnp.sum(logit_buf[block], axis=0))
+    scores = jnp.concatenate(sums, axis=1) * INVERSE_HEAT
     peak_mine = jnp.max(jnp.where(allowed, scores, NEG_LARGE), axis=1, keepdims=True)
     peak_buf[j] = jnp.broadcast_to(peak_mine, (2, 128))
     send_head(6, None, peak_buf)
@@ -447,20 +461,34 @@
         copy.wait()
     for phase, dst in enumerate(
         (
-            in_buf,
+            group_buf,
             pair_buf,
             mixer_buf,
             mixed_buf,
             out_buf,
-            logit_buf,
+            None,
             peak_buf,
             total_buf,
             square_buf,
             share_buf,
             scale_buf,
+            in_buf,
+            *[logit_buf.at[block] for block in range(4)],
         )
     ):
-        sent(phase, dst)
+        if dst is not None:
+            sent(phase, dst)
+
+
+def finish(*refs):
+    sems = refs[-1]
+    copies = [
+        pltpu.make_async_copy(refs[at], refs[at + 5], sems.at[at]) for at in range(5)
+    ]
+    for copy in copies:
+        copy.start()
+    for copy in copies:
+        copy.wait()
 
 
 def local(
@@ -486,15 +514,16 @@
 ):
     hbm = pl.BlockSpec(memory_space=pltpu.HBM)
     in_specs = [hbm] * N_IN
-    state, inner, group, out, probs = pl.pallas_call(
-        kernel,
-        out_shape=(
+    shapes = (
             jax.ShapeDtypeStruct((2, 8, 64, 256), BF),
             jax.ShapeDtypeStruct((3, 2, 512), BF),
             jax.ShapeDtypeStruct((3, 2, 128), BF),
             jax.ShapeDtypeStruct((ROWS, 512), BF),
             jax.ShapeDtypeStruct((2, 2048), BF),
-        ),
+    )
+    results = pl.pallas_call(
+        kernel,
+        out_shape=shapes,
         in_specs=in_specs,
         out_specs=(hbm,) * 5,
         scratch_shapes=[
@@ -524,24 +553,26 @@
             pltpu.SMEM((2,), jnp.int32),
             pltpu.VMEM((ROWS, 1, 512), F32),
             pltpu.VMEM((NR, 1, 128), F32),
-            pltpu.VMEM((NR, 2, 1280), F32),
-            pltpu.VMEM((NR, 2, 1280), F32),
-            pltpu.VMEM((NH, 2, 128), F32),
+            pltpu.VMEM((NR, 2, 128), F32),
+            pltpu.VMEM((NR, 2, 128), F32),
+            pltpu.VMEM((NR, 2, 1152), F32),
+            pltpu.VMEM((NR, 2, 1152), F32),
+            pltpu.VMEM((NH, 2, 128), BF),
             pltpu.VMEM((4, 2, 128), F32),
-            pltpu.VMEM((NR, 2, 512), F32),
+            pltpu.VMEM((NR, 2, 512), BF),
             pltpu.VMEM((ROWS, 1, 512), F32),
             pltpu.VMEM((NH, 1, 512), F32),
             pltpu.VMEM((NR, 1, 128), F32),
-            pltpu.VMEM((NH, 1, 640), F32),
-            pltpu.VMEM((NR, 2, 2048), F32),
-            pltpu.VMEM((NR, 2, 2048), F32),
+            pltpu.VMEM((NH, 2, 512), BF),
+            pltpu.VMEM((4, NR, 2, 512), F32),
+            pltpu.VMEM((4, NR, 2, 512), F32),
             pltpu.VMEM((NH, 2, 128), F32),
             pltpu.VMEM((NH, 2, 128), F32),
             pltpu.SemaphoreType.DMA((len(SMALL),)),
             pltpu.SemaphoreType.DMA((4,)),
             pltpu.SemaphoreType.DMA((5,)),
-            pltpu.SemaphoreType.DMA((11,)),
-            pltpu.SemaphoreType.DMA((11,)),
+            pltpu.SemaphoreType.DMA((16,)),
+            pltpu.SemaphoreType.DMA((16,)),
         ],
         compiler_params=pltpu.CompilerParams(
             collective_id=0, has_side_effects=True, vmem_limit_bytes=56 << 20
@@ -567,6 +598,14 @@
         token_mask,
         min_share,
     )
+    state, inner, group, out, probs = pl.pallas_call(
+        finish,
+        out_shape=shapes,
+        in_specs=[hbm] * 5,
+        out_specs=[hbm] * 5,
+        scratch_shapes=[pltpu.SemaphoreType.DMA((5,))],
+        compiler_params=pltpu.CompilerParams(vmem_limit_bytes=56 << 20),
+    )(*results)
     return (
         state,
         jnp.transpose(inner, (1, 0, 2)),

time: 88.9 us -> 95.3 us (1.072)
  Pallas kernels: 80.8 us -> 94.3 us
  local copies, waits for them, and re-layouts: 7.07 us -> 0 us
    pallas_call x1 -> x2, Pallas kernels: 80.8 us -> 94.3 us  [the longest x1 75.8 us: local(): pl.pallas_call(kernel, out_shape=shapes, in_specs=in_specs, out_specs=(hb...]
    unnamed x5 -> x0, local copies, waits for them, and re-layouts: 7.07 us -> none
where the time goes in v2:
time: 95.3 us; the launch traced here: 94.9 us
  Pallas kernels  94.3 us (99%)
    pallas_call x1, Pallas kernels, local(): pl.pallas_call(kernel, out_shape=shapes, in_specs=in_specs, out_specs=(hb...  75.8 us
    pallas_call x1, Pallas kernels, local(): pl.pallas_call(finish, out_shape=shapes, in_specs=[hbm] * 5, out_specs=[h...  18.5 us

profile of v2, /device:TPU:1, one launch (start us, length us, event | category | flops | bytes accessed | tf_op | source)
XLA Modules:
  0.0 94.9 jit_solution(16659928497174414990)
XLA Ops:
  0.6 75.8 %shard_map.218 = (bf16[2,8,64,256]{3,2,1,0:T(8,128)(2,1)}, bf16[3,2,512]{2,1,0:T(2,128)(2,1)}, bf16[3,2,128]{2,1,0:T(2,128)(2,1)}, bf16[32,512]{1,0:T(8,128)(2,1)}, bf16[2,2048]{1,0:T(2,128)(2,1)}) custom-call(bf16[32,512]{1,0:T(8,128)(2,1)} %hidden_h.1, bf16[512]{0:T(512)(128)(2,1)} %norm_gain_h.1, bf16[512,2,512]{2,1,0:T(2,128)(2,1)} %input_weight_h.1, ...), custom_call_target="tpu_custom_call" | custom-call | tf_op jit(solution)/shard_map/pallas_call | solution.py:524
  76.4 18.5 %shard_map.219 = (bf16[2,8,64,256]{3,2,1,0:T(8,128)(2,1)}, bf16[3,2,512]{2,1,0:T(2,128)(2,1)}, bf16[3,2,128]{2,1,0:T(2,128)(2,1)}, bf16[32,512]{1,0:T(8,128)(2,1)}, bf16[2,2048]{1,0:T(2,128)(2,1)}) custom-call(bf16[2,8,64,256]{3,2,1,0:T(8,128)(2,1)} %get-tuple-element.15.refs_0_, bf16[3,2,512]{2,1,0:T(2,128)(2,1)} %get-tuple-element.16.refs_1_, ...), custom_call_target="tpu_custom_call" | custom-call | tf_op jit(solution)/shard_map/pallas_call | solution.py:601

commit v3 on v2

--- a/solution.py
+++ b/solution.py
@@ -136,6 +136,24 @@
     i = lax.axis_index("row")
     j = lax.axis_index("head")
 
+    barrier = pltpu.get_barrier_semaphore()
+
+    def far_first(k, n):
+        return n // 2 + (2 * (k % 2) - 1) * ((k + 1) // 2)
+
+    def greet_row(k, carry):
+        to = lax.rem(i + far_first(k, NR), NR)
+        pl.semaphore_signal(barrier, inc=1, device_id=(to, j), device_id_type=MESH)
+        return carry
+
+    def greet_head(k, carry):
+        to = lax.rem(j + far_first(k, NH), NH)
+        pl.semaphore_signal(barrier, inc=1, device_id=(i, to), device_id_type=MESH)
+        return carry
+
+    lax.fori_loop(0, NR - 1, greet_row, 0)
+    lax.fori_loop(0, NH - 1, greet_head, 0)
+
     loads = {
         "hidden": (hidden_h, hidden_v),
         "norm_gain": (norm_gain_h, norm_gain_v),
@@ -174,24 +192,6 @@
         load_weight(block).start()
     for name in SMALL[2:]:
         load(name).start()
-
-    barrier = pltpu.get_barrier_semaphore()
-
-    def far_first(k, n):
-        return n // 2 + (2 * (k % 2) - 1) * ((k + 1) // 2)
-
-    def greet_row(k, carry):
-        to = lax.rem(i + far_first(k, NR), NR)
-        pl.semaphore_signal(barrier, inc=1, device_id=(to, j), device_id_type=MESH)
-        return carry
-
-    def greet_head(k, carry):
-        to = lax.rem(j + far_first(k, NH), NH)
-        pl.semaphore_signal(barrier, inc=1, device_id=(i, to), device_id_type=MESH)
-        return carry
-
-    lax.fori_loop(0, NR - 1, greet_row, 0)
-    lax.fori_loop(0, NH - 1, greet_head, 0)
 
     def send_row(phase, src, dst):
         def step(k, carry):
@@ -523,9 +523,9 @@
     )
     results = pl.pallas_call(
         kernel,
-        out_shape=shapes,
+        out_shape=tuple(pltpu.VMEM(shape.shape, BF) for shape in shapes),
         in_specs=in_specs,
-        out_specs=(hbm,) * 5,
+        out_specs=(pl.BlockSpec(memory_space=pltpu.VMEM),) * 5,
         scratch_shapes=[
             pltpu.VMEM((ROWS, 512), BF),
             pltpu.VMEM((512,), BF),
@@ -601,10 +601,10 @@
     state, inner, group, out, probs = pl.pallas_call(
         finish,
         out_shape=shapes,
-        in_specs=[hbm] * 5,
+        in_specs=[pl.BlockSpec(memory_space=pltpu.VMEM)] * 5,
         out_specs=[hbm] * 5,
         scratch_shapes=[pltpu.SemaphoreType.DMA((5,))],
-        compiler_params=pltpu.CompilerParams(vmem_limit_bytes=56 << 20),
+        compiler_params=pltpu.CompilerParams(vmem_limit_bytes=1 << 20),
     )(*results)
     return (
         state,

time: 95.3 us -> 77.1 us (0.81)
  Pallas kernels: 94.3 us -> 76 us
    pallas_call x2, Pallas kernels: 94.3 us -> 76 us  [the longest x1 75.2 us: local(): pl.pallas_call(kernel, out_shape=tuple((pltpu.VMEM(shape.shape, BF) for s...]
where the time goes in v3:
time: 77.1 us; the launch traced here: 76.7 us
  Pallas kernels  76 us (99%)
    pallas_call x1, Pallas kernels, local(): pl.pallas_call(kernel, out_shape=tuple((pltpu.VMEM(shape.shape, BF) for s...  75.2 us

profile of v3, /device:TPU:1, one launch (start us, length us, event | category | flops | bytes accessed | tf_op | source)
XLA Modules:
  0.0 76.7 jit_solution(9134508602833728468)
XLA Ops:
  0.6 75.2 %shard_map.218 = (bf16[2,8,64,256]{3,2,1,0:T(8,128)(2,1)S(1)}, bf16[3,2,512]{2,1,0:T(2,128)(2,1)S(1)}, bf16[3,2,128]{2,1,0:T(2,128)(2,1)S(1)}, bf16[32,512]{1,0:T(8,128)(2,1)S(1)}, bf16[2,2048]{1,0:T(2,128)(2,1)S(1)}) custom-call(bf16[32,512]{1,0:T(8,128)(2,1)} %hidden_h.1, bf16[512]{0:T(512)(128)(2,1)} %norm_gain_h.1, bf16[512,2,512]{2,1,0:T(2,128)(2,1)} %input_weight_h.1, ...), custom_call_target="tpu_custom_call" | custom-call | tf_op jit(solution)/shard_map/pallas_call | solution.py:524
  75.8 0.8 %shard_map.219 = (bf16[2,8,64,256]{3,2,1,0:T(8,128)(2,1)}, bf16[3,2,512]{2,1,0:T(2,128)(2,1)}, bf16[3,2,128]{2,1,0:T(2,128)(2,1)}, bf16[32,512]{1,0:T(8,128)(2,1)}, bf16[2,2048]{1,0:T(2,128)(2,1)}) custom-call(bf16[2,8,64,256]{3,2,1,0:T(8,128)(2,1)S(1)} %get-tuple-element.15.refs_0_, bf16[3,2,512]{2,1,0:T(2,128)(2,1)S(1)} %get-tuple-element.16.refs_1_, ...), custom_call_target="tpu_custom_call" | custom-call | tf_op jit(solution)/shard_map/pallas_call | solution.py:601

commit v4 on v3

--- a/solution.py
+++ b/solution.py
@@ -123,8 +123,12 @@
     mixed_buf,
     scale_buf,
     out_buf,
+    norm_buf,
     logit_part,
     logit_buf,
+    rest_part,
+    rest_buf,
+    main_rest,
     peak_buf,
     total_buf,
     in_sem,
@@ -267,7 +271,7 @@
     pl.semaphore_wait(barrier, NR + NH - 2)
     send_row(8, None, square_buf)
     arrived(8, square_buf)
-    square_total = jnp.sum(square_buf[:, 0, :], axis=0, keepdims=True)
+    square_total = jnp.sum(square_buf[...], axis=0)
     row_total = jnp.sum(jnp.where(diagonal, square_total, 0.0), axis=1, keepdims=True)
     hidden_scale = lax.rsqrt(row_total / D + EPSILON)
 
@@ -407,30 +411,47 @@
     load("final_gain").wait()
     final_gain_wide = final_gain_v[...].astype(F32).reshape(1, 512)
     arrived(3, mixed_buf)
-    mixed = jnp.sum(mixed_buf[:, 0, :], axis=0, keepdims=True)
-    out_rounded = (hidden_rows[j] + mixed).astype(BF)
-    out_mine = out_rounded.astype(F32)
+    mixed = jnp.sum(mixed_buf[...], axis=0)
+    out_mine = (hidden_rows[j] + mixed).astype(BF).astype(F32)
     scale_buf[i] = jnp.broadcast_to(jnp.sum(out_mine * out_mine, axis=1, keepdims=True), (1, 128))
     send_row(10, None, scale_buf)
+    out_buf[j] = out_mine
+    send_head(4, None, out_buf)
     arrived(10, scale_buf)
-    out_total = jnp.sum(scale_buf[:, 0, :], axis=0, keepdims=True)[:, 0:1]
-    out_scale = lax.rsqrt(out_total / D + EPSILON)
-    final_mine = (out_mine * out_scale * final_gain_wide).astype(BF).astype(F32)
-    out_buf[j] = jnp.concatenate([final_mine, out_mine], axis=0).astype(BF)
-    send_head(4, None, out_buf)
+    norm_buf[j] = lax.rsqrt(jnp.sum(scale_buf[...], axis=0) / D + EPSILON)
+    send_head(5, None, norm_buf)
 
     load("lexicon_matrix").wait()
     load("token_mask").wait()
     load("min_share").wait()
     arrived(4, out_buf)
-    final_rows = out_buf[:, 0, :]
-    for block in range(4):
-        at = slice(512 * block, 512 * block + 512)
-        logit_part[block] = dot(final_rows, lexicon_v[:, at]).reshape(NR, 2, 512)
+    out_wide = out_buf[:, 0, :]
+    scaled = out_wide * final_gain_wide
+    upper = scaled.astype(BF)
+    lower = (scaled - upper.astype(F32)).astype(BF)
+    exact_rows = jnp.concatenate([upper, lower], axis=0)
+    for block in range(2):
+        both = dot(exact_rows, lexicon_v[:, 1024 * block : 1024 * block + 1024])
+        main = both[:ROWS] + both[ROWS:]
+        coarse = main.astype(BF)
+        main_rest[block] = main - coarse.astype(F32)
+        logit_part[block] = coarse.reshape(NR, 2, 1024)
         send_row(12 + block, logit_part.at[block], logit_buf.at[block])
         logit_buf[block, i] = logit_part[block, i]
-    layer_out[...] = out_buf[:, 1, :]
+    layer_out[...] = out_wide.astype(BF)
     saves.append(save(3, layer_out, layer_out_h))
+
+    arrived(5, norm_buf)
+    row_scale = norm_buf[:, 0, :][:, 0:1]
+    normed_out = out_wide * row_scale * final_gain_wide
+    rounding = (normed_out.astype(BF).astype(F32) - normed_out).astype(BF)
+    for block in range(2):
+        rest = dot(rounding, lexicon_v[:, 1024 * block : 1024 * block + 1024])
+        rest = (rest + main_rest[block] * row_scale).astype(BF)
+        rest_part[block] = rest.reshape(NR, 2, 1024)
+        send_row(14 + block, rest_part.at[block], rest_buf.at[block])
+        rest_buf[block, i] = rest_part[block, i]
+    scale_mine = jnp.concatenate([norm_buf[2 * i], norm_buf[2 * i + 1]], axis=0)[:, 0:1]
 
     allowed = token_mask_v[...] > 0
     row_at = iota((2, 1), 0)
@@ -438,9 +459,12 @@
         jnp.where(row_at == 0, min_share[0], min_share[1]).astype(F32) / FIXED_POINT
     )
     sums = []
-    for block in range(4):
+    for block in range(2):
         arrived(12 + block, logit_buf.at[block])
-        sums.append(jnp.sum(logit_buf[block], axis=0))
+        sums.append(jnp.sum(logit_buf[block].astype(F32), axis=0) * scale_mine)
+    for block in range(2):
+        arrived(14 + block, rest_buf.at[block])
+        sums[block] += jnp.sum(rest_buf[block].astype(F32), axis=0)
     scores = jnp.concatenate(sums, axis=1) * INVERSE_HEAT
     peak_mine = jnp.max(jnp.where(allowed, scores, NEG_LARGE), axis=1, keepdims=True)
     peak_buf[j] = jnp.broadcast_to(peak_mine, (2, 128))
@@ -466,18 +490,18 @@
             mixer_buf,
             mixed_buf,
             out_buf,
-            None,
+            norm_buf,
             peak_buf,
             total_buf,
             square_buf,
             share_buf,
             scale_buf,
             in_buf,
-            *[logit_buf.at[block] for block in range(4)],
+            *[logit_buf.at[block] for block in range(2)],
+            *[rest_buf.at[block] for block in range(2)],
         )
     ):
-        if dst is not None:
-            sent(phase, dst)
+        sent(phase, dst)
 
 
 def finish(*refs):
@@ -563,9 +587,13 @@
             pltpu.VMEM((ROWS, 1, 512), F32),
             pltpu.VMEM((NH, 1, 512), F32),
             pltpu.VMEM((NR, 1, 128), F32),
-            pltpu.VMEM((NH, 2, 512), BF),
-            pltpu.VMEM((4, NR, 2, 512), F32),
-            pltpu.VMEM((4, NR, 2, 512), F32),
+            pltpu.VMEM((NH, 1, 512), F32),
+            pltpu.VMEM((NH, 1, 128), F32),
+            pltpu.VMEM((2, NR, 2, 1024), BF),
+            pltpu.VMEM((2, NR, 2, 1024), BF),
+            pltpu.VMEM((2, NR, 2, 1024), BF),
+            pltpu.VMEM((2, NR, 2, 1024), BF),
+            pltpu.VMEM((2, ROWS, 1024), F32),
             pltpu.VMEM((NH, 2, 128), F32),
             pltpu.VMEM((NH, 2, 128), F32),
             pltpu.SemaphoreType.DMA((len(SMALL),)),

time: 77.1 us -> 74.4 us (0.965)
  Pallas kernels: 76 us -> 73.6 us
    pallas_call x1, Pallas kernels: 75.2 us -> 72.8 us  [local(): pl.pallas_call(kernel, out_shape=tuple((pltpu.VMEM(shape.shape, BF) for s...]
where the time goes in v4:
time: 74.4 us; the launch traced here: 74.2 us
  Pallas kernels  73.6 us (99%)
    pallas_call x1, Pallas kernels, local(): pl.pallas_call(kernel, out_shape=tuple((pltpu.VMEM(shape.shape, BF) for s...  72.8 us

profile of v4, /device:TPU:1, one launch (start us, length us, event | category | flops | bytes accessed | tf_op | source)
XLA Modules:
  0.0 74.2 jit_solution(7741370494833501930)
XLA Ops:
  0.6 72.8 %shard_map.218 = (bf16[2,8,64,256]{3,2,1,0:T(8,128)(2,1)S(1)}, bf16[3,2,512]{2,1,0:T(2,128)(2,1)S(1)}, bf16[3,2,128]{2,1,0:T(2,128)(2,1)S(1)}, bf16[32,512]{1,0:T(8,128)(2,1)S(1)}, bf16[2,2048]{1,0:T(2,128)(2,1)S(1)}) custom-call(bf16[32,512]{1,0:T(8,128)(2,1)} %hidden_h.1, bf16[512]{0:T(512)(128)(2,1)} %norm_gain_h.1, bf16[512,2,512]{2,1,0:T(2,128)(2,1)} %input_weight_h.1, ...), custom_call_target="tpu_custom_call" | custom-call | tf_op jit(solution)/shard_map/pallas_call | solution.py:548
  73.4 0.8 %shard_map.219 = (bf16[2,8,64,256]{3,2,1,0:T(8,128)(2,1)}, bf16[3,2,512]{2,1,0:T(2,128)(2,1)}, bf16[3,2,128]{2,1,0:T(2,128)(2,1)}, bf16[32,512]{1,0:T(8,128)(2,1)}, bf16[2,2048]{1,0:T(2,128)(2,1)}) custom-call(bf16[2,8,64,256]{3,2,1,0:T(8,128)(2,1)S(1)} %get-tuple-element.15.refs_0_, bf16[3,2,512]{2,1,0:T(2,128)(2,1)S(1)} %get-tuple-element.16.refs_1_, ...), custom_call_target="tpu_custom_call" | custom-call | tf_op jit(solution)/shard_map/pallas_call | solution.py:629

commit v5 on v4

--- a/solution.py
+++ b/solution.py
@@ -110,6 +110,7 @@
     decay_log,
     skip_gain,
     min_share,
+    state_turned,
     hidden_rows,
     square_buf,
     group_part,
@@ -117,6 +118,7 @@
     in_part,
     in_buf,
     pair_buf,
+    share_mine,
     share_buf,
     mixer_buf,
     mixed_part,
@@ -128,7 +130,9 @@
     logit_buf,
     rest_part,
     rest_buf,
-    main_rest,
+    lexicon_lent,
+    exact_mine,
+    exact_lent,
     peak_buf,
     total_buf,
     in_sem,
@@ -172,7 +176,10 @@
         "token_mask": (token_mask_h, token_mask_v),
         "recurrent_state": (recurrent_state_h, recurrent_state_v),
         "output_weight": (output_weight_h, output_weight_v),
-        "lexicon_matrix": (lexicon_h, lexicon_v),
+        "lexicon_matrix": (
+            lexicon_h.at[:, pl.ds(pl.multiple_of((i % 2) * 1024, 1024), 1024)],
+            lexicon_v,
+        ),
         "timestep_bias": (timestep_bias_h, timestep_bias),
         "decay_log": (decay_log_h, decay_log),
         "skip_gain": (skip_gain_h, skip_gain),
@@ -235,28 +242,63 @@
         rest = dst.at[pl.ds(0, dst.shape[0] - 1)]
         pltpu.make_async_copy(rest, rest, send_sem.at[phase]).wait()
 
-    def send_group(phase, dst):
-        first = j - j % 4
-
+    sibling = i + 1 - 2 * (i % 2)
+    half_slot = (i % 2) * 8 + i // 2
+
+    def to_sibling(phase, src, dst):
+        return pltpu.make_async_remote_copy(
+            src_ref=src,
+            dst_ref=dst,
+            send_sem=send_sem.at[phase],
+            recv_sem=recv_sem.at[phase],
+            device_id=(sibling, j),
+            device_id_type=MESH,
+        )
+
+    lend_lexicon = to_sibling(
+        14,
+        lexicon_h.at[:, pl.ds(pl.multiple_of((1 - i % 2) * 1024, 1024), 1024)],
+        lexicon_lent,
+    )
+
+    def send_half(phase, src, dst):
         def step(k, carry):
-            to = first + lax.rem(j + k, 4)
+            to = lax.rem(i + far_first(k, NR), NR)
             pltpu.make_async_remote_copy(
-                src_ref=dst.at[j % 4],
-                dst_ref=dst.at[j % 4],
+                src_ref=src.at[to],
+                dst_ref=dst.at[half_slot],
                 send_sem=send_sem.at[phase],
                 recv_sem=recv_sem.at[phase],
-                device_id=(i, to),
+                device_id=(to, j),
                 device_id_type=MESH,
             ).start()
             return carry
 
-        lax.fori_loop(1, 4, step, 0)
+        lax.fori_loop(0, NR - 1, step, 0)
+
+    column = (j % 4) * NR
+
+    def send_across(phase, src, dst):
+        def step(k, carry):
+            to = (lax.rem(i + 8 + k // 3, NR), j - j % 4 + lax.rem(j + 1 + k % 3, 4))
+            pltpu.make_async_remote_copy(
+                src_ref=src,
+                dst_ref=dst.at[column + i],
+                send_sem=send_sem.at[phase],
+                recv_sem=recv_sem.at[phase],
+                device_id=to,
+                device_id_type=MESH,
+            ).start()
+            return carry
+
+        lax.fori_loop(0, 3 * NR, step, 0)
 
     def save(at, src, dst):
         copy = pltpu.make_async_copy(src, dst, save_sem.at[at])
         copy.start()
         return copy
 
+    share_buf[pl.ds(column, NR)] = jnp.zeros((NR, 2, 128), F32)
     load("hidden").wait()
     load("norm_gain").wait()
     hidden_wide = hidden_v[...].astype(F32)
@@ -270,6 +312,9 @@
     load("group_weight").wait()
     pl.semaphore_wait(barrier, NR + NH - 2)
     send_row(8, None, square_buf)
+    load("recurrent_state").wait()
+    for r in range(2):
+        state_turned[r] = recurrent_state_v[r].reshape(512, 256).T
     arrived(8, square_buf)
     square_total = jnp.sum(square_buf[...], axis=0)
     row_total = jnp.sum(jnp.where(diagonal, square_total, 0.0), axis=1, keepdims=True)
@@ -314,6 +359,7 @@
     )
     pair_buf[j] = silu(group_mix).astype(BF)
     send_head(1, None, pair_buf)
+    lend_lexicon.start()
 
     next_conv_group[0] = conv_group_state_v[1]
     next_conv_group[1] = conv_group_state_v[2]
@@ -357,7 +403,6 @@
     channel_at, entry_at = iota((128, 256), 0), iota((128, 256), 1)
     pick = (channel_at == (entry_at % 16) * GROUPS + group_at).astype(F32).astype(BF)
     source_at, entry_of = iota((NH, 256), 0), iota((NH, 256), 1) // 16
-    load("recurrent_state").wait()
     load("mixer_gain").wait()
     arrived(1, pair_buf)
     inputs, readouts = [], []
@@ -371,7 +416,7 @@
         )
     readout = []
     for r in range(2):
-        old_read = dot_nt(readouts[r].astype(BF), recurrent_state_v[r].reshape(512, 256))
+        old_read = dot(readouts[r].astype(BF), state_turned[r])
         pair_dot = jnp.sum(inputs[r] * readouts[r], axis=1, keepdims=True)
         readout.append(
             decay[r : r + 1] * old_read
@@ -381,13 +426,11 @@
     gated = jnp.concatenate(readout, axis=0) * gate
     gated_squares = jnp.sum(gated * gated, axis=1, keepdims=True)
     mixer_gain_wide = mixer_gain_v[...].astype(F32).reshape(1, 512)
-    share_buf[j % 4] = jnp.broadcast_to(gated_squares, (2, 128))
-    send_group(9, share_buf)
-    arrived(9, share_buf)
-    group_total = jnp.sum(share_buf[...], axis=0)[:, 0:1]
-    group_scale = lax.rsqrt(group_total / (HEADS * HEAD_DIM // GROUPS) + EPSILON)
-    mixer_buf[i] = (gated * group_scale * mixer_gain_wide).astype(BF)
+    mixer_buf[i, :, 0:512] = gated
+    mixer_buf[i, :, 512:640] = jnp.broadcast_to(gated_squares, (2, 128))
+    share_mine[...] = jnp.broadcast_to(gated_squares, (2, 128))
     send_row(2, None, mixer_buf)
+    send_across(9, share_mine, share_buf)
 
     rows8 = jnp.concatenate([driven, decay, jnp.zeros((4, 512), F32)], axis=0)
     columns = rows8.T
@@ -403,7 +446,14 @@
 
     load("output_weight").wait()
     arrived(2, mixer_buf)
-    mixer_rows = mixer_buf[...].reshape(ROWS, 512)
+    rest = share_buf.at[pl.ds(0, 3 * NR)]
+    pltpu.make_async_copy(rest, rest, recv_sem.at[9]).wait()
+    group_total = mixer_buf[:, :, 512:640]
+    for at in range(4):
+        group_total += share_buf[NR * at : NR * at + NR]
+    group_scale = lax.rsqrt(group_total / (HEADS * HEAD_DIM // GROUPS) + EPSILON)[:, :, 0:1]
+    mixer_rows = (mixer_buf[:, :, 0:512] * group_scale * mixer_gain_wide).astype(BF)
+    mixer_rows = mixer_rows.reshape(ROWS, 512)
     mixed_part[:, 0, :] = dot(mixer_rows, output_weight_v[...])
     send_head(3, mixed_part, mixed_buf)
     mixed_buf[j] = mixed_part[j]
@@ -429,28 +479,35 @@
     scaled = out_wide * final_gain_wide
     upper = scaled.astype(BF)
     lower = (scaled - upper.astype(F32)).astype(BF)
-    exact_rows = jnp.concatenate([upper, lower], axis=0)
-    for block in range(2):
-        both = dot(exact_rows, lexicon_v[:, 1024 * block : 1024 * block + 1024])
-        main = both[:ROWS] + both[ROWS:]
-        coarse = main.astype(BF)
-        main_rest[block] = main - coarse.astype(F32)
-        logit_part[block] = coarse.reshape(NR, 2, 1024)
-        send_row(12 + block, logit_part.at[block], logit_buf.at[block])
-        logit_buf[block, i] = logit_part[block, i]
+    exact_mine[0:ROWS] = upper
+    exact_mine[ROWS:] = lower
+    lend_rows = to_sibling(15, exact_mine, exact_lent)
+    lend_rows.start()
+    both = dot(exact_mine[...], lexicon_v[...])
+    lend_lexicon.wait()
+    lend_rows.wait()
+    both += dot(exact_lent[...], lexicon_lent[...])
+    main = both[:ROWS] + both[ROWS:]
+    coarse = main.astype(BF)
+    logit_part[...] = coarse.reshape(NR, 2, 1024)
+    send_half(12, logit_part, logit_buf)
+    logit_buf[half_slot] = logit_part[i]
+    main_rest = main - coarse.astype(F32)
+    scaled_lent = exact_lent[0:ROWS].astype(F32) + exact_lent[ROWS:].astype(F32)
     layer_out[...] = out_wide.astype(BF)
     saves.append(save(3, layer_out, layer_out_h))
 
     arrived(5, norm_buf)
     row_scale = norm_buf[:, 0, :][:, 0:1]
-    normed_out = out_wide * row_scale * final_gain_wide
-    rounding = (normed_out.astype(BF).astype(F32) - normed_out).astype(BF)
-    for block in range(2):
-        rest = dot(rounding, lexicon_v[:, 1024 * block : 1024 * block + 1024])
-        rest = (rest + main_rest[block] * row_scale).astype(BF)
-        rest_part[block] = rest.reshape(NR, 2, 1024)
-        send_row(14 + block, rest_part.at[block], rest_buf.at[block])
-        rest_buf[block, i] = rest_part[block, i]
+
+    def rounding(product):
+        exact = product * row_scale
+        return (exact.astype(BF).astype(F32) - exact).astype(BF)
+
+    rest = dot(rounding(scaled), lexicon_v[...]) + dot(rounding(scaled_lent), lexicon_lent[...])
+    rest_part[...] = (rest + main_rest * row_scale).astype(BF).reshape(NR, 2, 1024)
+    send_half(13, rest_part, rest_buf)
+    rest_buf[half_slot] = rest_part[i]
     scale_mine = jnp.concatenate([norm_buf[2 * i], norm_buf[2 * i + 1]], axis=0)[:, 0:1]
 
     allowed = token_mask_v[...] > 0
@@ -458,14 +515,20 @@
     floor_share = (
         jnp.where(row_at == 0, min_share[0], min_share[1]).astype(F32) / FIXED_POINT
     )
-    sums = []
-    for block in range(2):
-        arrived(12 + block, logit_buf.at[block])
-        sums.append(jnp.sum(logit_buf[block].astype(F32), axis=0) * scale_mine)
-    for block in range(2):
-        arrived(14 + block, rest_buf.at[block])
-        sums[block] += jnp.sum(rest_buf[block].astype(F32), axis=0)
-    scores = jnp.concatenate(sums, axis=1) * INVERSE_HEAT
+
+    def half_sums(buf):
+        return jnp.concatenate(
+            [
+                jnp.sum(buf[0:8].astype(F32), axis=0),
+                jnp.sum(buf[8:16].astype(F32), axis=0),
+            ],
+            axis=1,
+        )
+
+    arrived(12, logit_buf)
+    main_sum = half_sums(logit_buf) * scale_mine
+    arrived(13, rest_buf)
+    scores = (main_sum + half_sums(rest_buf)) * INVERSE_HEAT
     peak_mine = jnp.max(jnp.where(allowed, scores, NEG_LARGE), axis=1, keepdims=True)
     peak_buf[j] = jnp.broadcast_to(peak_mine, (2, 128))
     send_head(6, None, peak_buf)
@@ -494,11 +557,11 @@
             peak_buf,
             total_buf,
             square_buf,
-            share_buf,
+            share_buf.at[pl.ds(0, 3 * NR + 1)],
             scale_buf,
             in_buf,
-            *[logit_buf.at[block] for block in range(2)],
-            *[rest_buf.at[block] for block in range(2)],
+            logit_buf,
+            rest_buf,
         )
     ):
         sent(phase, dst)
@@ -564,7 +627,7 @@
             pltpu.VMEM((512,), BF),
             pltpu.VMEM((512, 512), BF),
             pltpu.VMEM((512,), BF),
-            pltpu.VMEM((512, 2048), BF),
+            pltpu.VMEM((512, 1024), BF),
             pltpu.VMEM((2, 2048), jnp.int32),
             pltpu.VMEM((2, 8, 64, 256), BF),
             pltpu.VMEM((3, 2, 512), BF),
@@ -575,6 +638,7 @@
             pltpu.SMEM((8,), F32),
             pltpu.SMEM((8,), F32),
             pltpu.SMEM((2,), jnp.int32),
+            pltpu.VMEM((2, 256, 512), BF),
             pltpu.VMEM((ROWS, 1, 512), F32),
             pltpu.VMEM((NR, 1, 128), F32),
             pltpu.VMEM((NR, 2, 128), F32),
@@ -582,18 +646,21 @@
             pltpu.VMEM((NR, 2, 1152), F32),
             pltpu.VMEM((NR, 2, 1152), F32),
             pltpu.VMEM((NH, 2, 128), BF),
-            pltpu.VMEM((4, 2, 128), F32),
-            pltpu.VMEM((NR, 2, 512), BF),
+            pltpu.VMEM((2, 128), F32),
+            pltpu.VMEM((4 * NR, 2, 128), F32),
+            pltpu.VMEM((NR, 2, 640), F32),
             pltpu.VMEM((ROWS, 1, 512), F32),
             pltpu.VMEM((NH, 1, 512), F32),
             pltpu.VMEM((NR, 1, 128), F32),
             pltpu.VMEM((NH, 1, 512), F32),
             pltpu.VMEM((NH, 1, 128), F32),
-            pltpu.VMEM((2, NR, 2, 1024), BF),
-            pltpu.VMEM((2, NR, 2, 1024), BF),
-            pltpu.VMEM((2, NR, 2, 1024), BF),
-            pltpu.VMEM((2, NR, 2, 1024), BF),
-            pltpu.VMEM((2, ROWS, 1024), F32),
+            pltpu.VMEM((NR, 2, 1024), BF),
+            pltpu.VMEM((NR, 2, 1024), BF),
+            pltpu.VMEM((NR, 2, 1024), BF),
+            pltpu.VMEM((NR, 2, 1024), BF),
+            pltpu.VMEM((512, 1024), BF),
+            pltpu.VMEM((2 * ROWS, 512), BF),
+            pltpu.VMEM((2 * ROWS, 512), BF),
             pltpu.VMEM((NH, 2, 128), F32),
             pltpu.VMEM((NH, 2, 128), F32),
             pltpu.SemaphoreType.DMA((len(SMALL),)),

time: 74.4 us -> 72.7 us (0.977)
  Pallas kernels: 73.6 us -> 71.9 us
    pallas_call x1, Pallas kernels: 72.8 us -> 71.1 us  [local(): pl.pallas_call(kernel, out_shape=tuple((pltpu.VMEM(shape.shape, BF) for s...]
where the time goes in v5:
time: 72.7 us; the launch traced here: 72.6 us
  Pallas kernels  71.9 us (99%)
    pallas_call x1, Pallas kernels, local(): pl.pallas_call(kernel, out_shape=tuple((pltpu.VMEM(shape.shape, BF) for s...  71.1 us

profile of v5, /device:TPU:1, one launch (start us, length us, event | category | flops | bytes accessed | tf_op | source)
XLA Modules:
  0.0 72.6 jit_solution(3241158571415064695)
XLA Ops:
  0.6 71.1 %shard_map.218 = (bf16[2,8,64,256]{3,2,1,0:T(8,128)(2,1)S(1)}, bf16[3,2,512]{2,1,0:T(2,128)(2,1)S(1)}, bf16[3,2,128]{2,1,0:T(2,128)(2,1)S(1)}, bf16[32,512]{1,0:T(8,128)(2,1)S(1)}, bf16[2,2048]{1,0:T(2,128)(2,1)S(1)}) custom-call(bf16[32,512]{1,0:T(8,128)(2,1)} %hidden_h.1, bf16[512]{0:T(512)(128)(2,1)} %norm_gain_h.1, bf16[512,2,512]{2,1,0:T(2,128)(2,1)} %input_weight_h.1, ...), custom_call_target="tpu_custom_call" | custom-call | tf_op jit(solution)/shard_map/pallas_call | solution.py:611
  71.7 0.8 %shard_map.219 = (bf16[2,8,64,256]{3,2,1,0:T(8,128)(2,1)}, bf16[3,2,512]{2,1,0:T(2,128)(2,1)}, bf16[3,2,128]{2,1,0:T(2,128)(2,1)}, bf16[32,512]{1,0:T(8,128)(2,1)}, bf16[2,2048]{1,0:T(2,128)(2,1)}) custom-call(bf16[2,8,64,256]{3,2,1,0:T(8,128)(2,1)S(1)} %get-tuple-element.15.refs_0_, bf16[3,2,512]{2,1,0:T(2,128)(2,1)S(1)} %get-tuple-element.16.refs_1_, ...), custom_call_target="tpu_custom_call" | custom-call | tf_op jit(solution)/shard_map/pallas_call | solution.py:696

commit v6 on v5

--- a/solution.py
+++ b/solution.py
@@ -140,6 +140,7 @@
     save_sem,
     send_sem,
     recv_sem,
+    column_sem,
 ):
     i = lax.axis_index("row")
     j = lax.axis_index("head")
@@ -154,13 +155,11 @@
         pl.semaphore_signal(barrier, inc=1, device_id=(to, j), device_id_type=MESH)
         return carry
 
-    def greet_head(k, carry):
-        to = lax.rem(j + far_first(k, NH), NH)
+    lax.fori_loop(0, NR - 1, greet_row, 0)
+    offsets = (1 + i, 17 + i - i // 15)
+    for offset in offsets:
+        to = lax.rem(j + offset, NH)
         pl.semaphore_signal(barrier, inc=1, device_id=(i, to), device_id_type=MESH)
-        return carry
-
-    lax.fori_loop(0, NR - 1, greet_row, 0)
-    lax.fori_loop(0, NH - 1, greet_head, 0)
 
     loads = {
         "hidden": (hidden_h, hidden_v),
@@ -280,7 +279,7 @@
 
     def send_across(phase, src, dst):
         def step(k, carry):
-            to = (lax.rem(i + 8 + k // 3, NR), j - j % 4 + lax.rem(j + 1 + k % 3, 4))
+            to = (lax.rem(i + far_first(k // 3, NR), NR), j - j % 4 + lax.rem(j + 1 + k % 3, 4))
             pltpu.make_async_remote_copy(
                 src_ref=src,
                 dst_ref=dst.at[column + i],
@@ -310,8 +309,11 @@
     spread_even = (slot_at == 2 * depth_at).astype(F32).astype(BF)
     spread_odd = (slot_at == 2 * depth_at + 1).astype(F32).astype(BF)
     load("group_weight").wait()
-    pl.semaphore_wait(barrier, NR + NH - 2)
+    pl.semaphore_wait(barrier, NR + 1)
     send_row(8, None, square_buf)
+    for offset in offsets:
+        to = lax.rem(j + NH - offset, NH)
+        pl.semaphore_signal(column_sem, inc=1, device_id=(i, to), device_id_type=MESH)
     load("recurrent_state").wait()
     for r in range(2):
         state_turned[r] = recurrent_state_v[r].reshape(512, 256).T
@@ -322,6 +324,7 @@
 
     gained = (hidden_wide * hidden_scale * norm_gain_v[...].astype(F32).reshape(1, 512)).astype(BF)
     group_part[...] = dot(gained, group_weight_v[...]).reshape(NR, 2, 128)
+    pl.semaphore_wait(column_sem, 2)
     send_row(0, group_part, group_buf)
     group_buf[i] = group_part[i]
     blocks = [gained[:, 128 * b : 128 * b + 128] for b in range(4)]
@@ -668,6 +671,7 @@
             pltpu.SemaphoreType.DMA((5,)),
             pltpu.SemaphoreType.DMA((16,)),
             pltpu.SemaphoreType.DMA((16,)),
+            pltpu.SemaphoreType.REGULAR,
         ],
         compiler_params=pltpu.CompilerParams(
             collective_id=0, has_side_effects=True, vmem_limit_bytes=56 << 20

time: 72.7 us -> 72.1 us (level)
  Pallas kernels: 71.9 us -> 71 us
    pallas_call x1, Pallas kernels: 71.1 us -> 70.1 us  [local(): pl.pallas_call(kernel, out_shape=tuple((pltpu.VMEM(shape.shape, BF) for s...]
where the time goes in v6:
time: 72.1 us; the launch traced here: 71.6 us
  Pallas kernels  71 us (98%)
    pallas_call x1, Pallas kernels, local(): pl.pallas_call(kernel, out_shape=tuple((pltpu.VMEM(shape.shape, BF) for s...  70.1 us

profile of v6, /device:TPU:1, one launch (start us, length us, event | category | flops | bytes accessed | tf_op | source)
XLA Modules:
  0.0 71.6 jit_solution(5717995841183190700)
XLA Ops:
  0.6 70.1 %shard_map.218 = (bf16[2,8,64,256]{3,2,1,0:T(8,128)(2,1)S(1)}, bf16[3,2,512]{2,1,0:T(2,128)(2,1)S(1)}, bf16[3,2,128]{2,1,0:T(2,128)(2,1)S(1)}, bf16[32,512]{1,0:T(8,128)(2,1)S(1)}, bf16[2,2048]{1,0:T(2,128)(2,1)S(1)}) custom-call(bf16[32,512]{1,0:T(8,128)(2,1)} %hidden_h.1, bf16[512]{0:T(512)(128)(2,1)} %norm_gain_h.1, bf16[512,2,512]{2,1,0:T(2,128)(2,1)} %input_weight_h.1, ...), custom_call_target="tpu_custom_call" | custom-call | tf_op jit(solution)/shard_map/pallas_call | solution.py:614
  70.8 0.8 %shard_map.219 = (bf16[2,8,64,256]{3,2,1,0:T(8,128)(2,1)}, bf16[3,2,512]{2,1,0:T(2,128)(2,1)}, bf16[3,2,128]{2,1,0:T(2,128)(2,1)}, bf16[32,512]{1,0:T(8,128)(2,1)}, bf16[2,2048]{1,0:T(2,128)(2,1)}) custom-call(bf16[2,8,64,256]{3,2,1,0:T(8,128)(2,1)S(1)} %get-tuple-element.15.refs_0_, bf16[3,2,512]{2,1,0:T(2,128)(2,1)S(1)} %get-tuple-element.16.refs_1_, ...), custom_call_target="tpu_custom_call" | custom-call | tf_op jit(solution)/shard_map/pallas_call | solution.py:700
